TPU v7x, 32 devices: a whole 2x2x4 slice. The times are simulated.
32 devices in a mesh: gx: 2 (over x), gy: 4 (over y, core), gz: 4 (over z).
Axes of the slice: x: 2, y: 2, z: 4, core: 2. Of those that a mesh axis runs over, the one named last changes fastest.
Arguments:
- solid_state: float32 [9, 32, 16, 512], P(None, 'gz', 'gx', 'gy'), may hold values from -6 to 6
- material: float32 [4, 32, 16, 512], P(None, 'gz', 'gx', 'gy'), may hold values from 0.5 to 2
- ocean_state: float32 [4, 16, 32, 1024], P(None, None, 'gx', ('gy', 'gz')), may hold values from -6 to 6
- ocean_medium: float32 [2, 16], replicated, may hold values from 0.5 to 2
- offset_x: int32 [32], P('gx'), may hold values from -1 to 1
- offset_y: int32 [1024], P(('gy', 'gz')), may hold values from -1 to 1
Outputs:
- solid_next: float32 [9, 32, 16, 512], P(None, 'gz', 'gx', 'gy')
- solid_rate: float32 [9, 32, 16, 512], P(None, 'gz', 'gx', 'gy')
- ocean_next: float32 [4, 16, 32, 1024], P(None, None, 'gx', ('gy', 'gz'))
- ocean_rate: float32 [4, 16, 32, 1024], P(None, None, 'gx', ('gy', 'gz'))
All inputs are finite; a program needn't handle non-finite values.
Results may differ from a plain program's by a relative error of at most 0.000059.
Values sent between devices are 32-bit elements; how exact they have to be, the bound alone decides.
No kernel may reach another device: no remote copies, remote signals or barrier semaphores. Data moves between devices by JAX's collectives and lax.ppermute only.
A program may use at most 64 MiB of HBM per device.

v0:
```python
import functools

import jax
import jax.numpy as jnp
from jax import lax
from jax.experimental import pallas as pl
from jax.experimental.pallas import tpu as pltpu
from jax.sharding import PartitionSpec as P


closure_rows = (
    (-24.0 / 17.0, 59.0 / 34.0, -4.0 / 17.0, -3.0 / 34.0, 0.0, 0.0),
    (-0.5, 0.0, 0.5, 0.0, 0.0, 0.0),
    (4.0 / 43.0, -59.0 / 86.0, 0.0, 59.0 / 86.0, -4.0 / 43.0, 0.0),
    (3.0 / 98.0, 0.0, -59.0 / 98.0, 0.0, 32.0 / 49.0, -4.0 / 49.0),
)
inv_norm = 48.0 / 17.0
step_size = 0.25
section_weight = 0.1496590219993
gravity = 0.4
interior_weights = {-2: 1.0 / 12.0, -1: -8.0 / 12.0, 1: 8.0 / 12.0, 2: -1.0 / 12.0}

x_fields = (0, 1, 2, 3, 8, 7)
y_fields = (0, 1, 2, 4, 8, 6)
z_fields = (0, 1, 2, 5, 6, 7)
ocean_x_fields = (1, 0)
ocean_y_fields = (2, 0)
rows, lanes, half = 8, 128, 64
far = 1 << 20


def turn(x, shift, axis):
    shift = shift % x.shape[axis]
    return x if shift == 0 else pltpu.roll(x, shift, axis)


def flag(value, shape=(rows, lanes)):
    return jnp.broadcast_to(value.astype(jnp.int32), shape) == 1


def lane_of(shape=(rows, lanes)):
    return lax.broadcasted_iota(jnp.int32, shape, 1)


def row_of(shape=(rows, lanes)):
    return lax.broadcasted_iota(jnp.int32, shape, 0)


def stencil(position, extent, first, last):
    low = position + far * (1 - first)
    high = extent - 1 - position + far * (1 - last)
    plain = jnp.logical_and(low >= 4, high >= 4)
    weights = {}
    for s in range(-3, 4):
        inside = jnp.logical_and(position + s >= 0, position + s < extent)
        w = jnp.where(jnp.logical_and(inside, plain), interior_weights.get(s, 0.0), 0.0)
        for r in range(4):
            if 0 <= r + s < 6 and closure_rows[r][r + s] != 0.0:
                w = jnp.where(low == r, closure_rows[r][r + s], w)
            if 0 <= r - s < 6 and closure_rows[r][r - s] != 0.0:
                w = jnp.where(high == r, -closure_rows[r][r - s], w)
        weights[s] = w
    return weights


def slope(x, weights, axis):
    total = weights[0] * x
    for s in (-3, -2, -1, 1, 2, 3):
        total = total + weights[s] * turn(x, -s, axis)
    return total


def pack_edges(tiles):
    group = lax.shift_right_logical(lane_of(), 2)
    out = []
    for start in range(0, len(tiles), 32):
        acc = jnp.zeros((rows, lanes), jnp.float32)
        for q, tile in enumerate(tiles[start : start + 32]):
            acc = jnp.where(group == q, turn(tile, 4 * q + 2, 1), acc)
        out.append(acc)
    return out


def edge_terms(left, right, has_left, has_right):
    place = jnp.bitwise_and(lane_of(), 3)
    low = jnp.where(
        place == 2, turn(left, 2, 1) - 8.0 * turn(left, 1, 1), turn(left, 2, 1)
    )
    high = jnp.where(
        place == 0, -turn(right, -2, 1), 8.0 * turn(right, -1, 1) - turn(right, -2, 1)
    )
    low = jnp.where(has_left, low, 0.0)
    high = jnp.where(has_right, high, 0.0)
    return jnp.where(place >= 2, low, high) * (1.0 / 12.0)


def row_terms(pack, from_low):
    even = jnp.bitwise_and(row_of(), 1) == 0
    low = jnp.where(even, pack - 8.0 * turn(pack, -1, 0), pack)
    high = jnp.where(even, -pack, 8.0 * turn(pack, 1, 0) - pack)
    return jnp.where(from_low, low, turn(high, 6, 0)) * (1.0 / 12.0)


def pair_rounds(size):
    first = [(i, i ^ 1) for i in range(size)]
    if size == 2:
        return (first,)
    second = [(i, (i + 1) % size if i % 2 else (i - 1) % size) for i in range(size)]
    return (first, second)


def where_am_i():
    return lax.axis_index("gx"), lax.axis_index("gy"), lax.axis_index("gz")


def paired_level(ocean, field, k, levels):
    a = ocean[field, k]
    b = ocean[field, k + levels // 2]
    return jnp.concatenate([a, b], axis=1)


def row_rims(planes):
    if len(planes) == 1:
        return jnp.concatenate([planes[0][-1:], planes[0][:1]], axis=0)
    odd = lax.axis_index("gx") % 2 == 1
    low = jnp.where(odd, planes[0][-1:], planes[1][-1:])
    high = jnp.where(odd, planes[1][:1], planes[0][:1])
    return jnp.concatenate([low, high], axis=0)


def rim_tile_of(planes):
    odd = flag(lax.rem(lax.axis_index("gx"), 2))
    low, high = sides([plane[...] for plane in planes], odd)
    rim = jnp.where(row_of() == 0, turn(low, 1, 0), turn(high, 1, 0))
    return jnp.where(row_of() < 2, rim, 0.0)


def sides(got, odd):
    if len(got) == 1:
        return got[0], got[0]
    return jnp.where(odd, got[0], got[1]), jnp.where(odd, got[1], got[0])


def one(condition):
    return condition.astype(jnp.int32)


def run_copies(copies):
    for copy in copies:
        copy.start()


def stage_kernel(sizes, *refs):
    solid_far, ocean_far, medium_far, offset_x_far, offset_y_far = refs[:5]
    solid, ocean, medium, index = refs[5:9]
    small, offset_x, offset_y, sems = refs[9:]
    copies = [
        pltpu.make_async_copy(solid_far, solid, sems.at[0]),
        pltpu.make_async_copy(ocean_far, ocean, sems.at[1]),
        pltpu.make_async_copy(medium_far, small, sems.at[2]),
        pltpu.make_async_copy(offset_x_far, offset_x, sems.at[3]),
        pltpu.make_async_copy(offset_y_far, offset_y, sems.at[4]),
    ]
    run_copies(copies)
    for copy in copies[2:]:
        copy.wait()
    fill_tables(sizes, small, offset_x, offset_y, medium, index)
    for copy in copies[:2]:
        copy.wait()


def pack_x_kernel(solid, ocean, *outs):
    levels, fine = ocean.shape[1:3]
    depth = solid.shape[1]
    odd = flag(lax.rem(lax.axis_index("gx"), 2))
    pair = lax.shift_right_logical(row_of(), 1)

    def emit(heads, base):
        for number, out in enumerate(outs):
            acc = None
            for t, (head, tail) in enumerate(heads):
                q = t % 4
                edge = jnp.where(odd, head, tail) if number == 0 else jnp.where(odd, tail, head)
                edge = turn(edge, 2 * q, 0)
                acc = edge if q == 0 else jnp.where(pair == q, edge, acc)
                if q == 3:
                    out[base + t // 4] = acc

    heads = []
    for field in x_fields:
        for k in range(depth):
            tile = solid[field, k]
            heads.append((tile, turn(tile, 2, 0)))
    emit(heads, 0)
    base = len(heads) // 4
    heads = []
    for field in ocean_x_fields:
        for k in range(levels // 2):
            tile = paired_level(ocean, field, k, levels)
            heads.append((tile[:rows], turn(tile[fine - rows :], 2, 0)))
    emit(heads, base)


def pack_kernel(solid, ocean, out_y, out_small, out_even, out_odd, out_pressure):
    levels, fine, width = ocean.shape[1:]
    depth = solid.shape[1]
    _, _, z = where_am_i()
    odd_z = lax.rem(z, 2)
    zero = jnp.zeros((rows, lanes), jnp.float32)
    packed = pack_edges([solid[field, k] for field in y_fields for k in range(depth)])
    outer, inner = [], []
    for field in ocean_y_fields:
        for k in range(levels // 2):
            tile = paired_level(ocean, field, k, levels)
            for r in range(0, fine, rows):
                outer.append(tile[r : r + rows])
                inner.append(turn(tile[r : r + rows], half, 1))
    ends = pack_edges(outer) + pack_edges(inner)
    for i, tile in enumerate(packed + ends + [zero]):
        out_y[i] = tile
    start_even = (1 - odd_z) * (depth - 2)
    start_odd = odd_z * (depth - 2)
    count = 0
    for field in z_fields:
        for k in range(2):
            out_even[count] = solid[field, start_even + k]
            out_odd[count] = solid[field, start_odd + k]
            count += 1
    for i, tile in enumerate(ends):
        out_small[i] = tile
        out_odd[count + i] = tile

    deepest = ocean[0, levels - 1]
    deepest = jnp.concatenate([deepest, deepest], axis=1)
    source = jnp.bitwise_and(2 * row_of(), rows - 1)
    halves = []
    for r in range(2):
        part = deepest[r * rows : (r + 1) * rows]
        halves.append(pick(part + turn(part, -1, 0), source, 0))
    pressure = jnp.where(row_of() < rows // 2, halves[0], halves[1])
    pressure = 0.25 * (pressure + turn(pressure, -1, 1))
    column = lane_of() - z * (width // 2)
    mine = jnp.logical_and(column >= 0, column < width // 2)
    pressure = pick(pressure, jnp.bitwise_and(2 * column, lanes - 1), 1)
    pressure = jnp.where(mine, pressure, 0.0)
    out_pressure[0] = pressure
    out_small[2] = jnp.where(flag(one(z == 0)), solid[2, 0], pressure)
    out_small[3] = zero


def fill_tables(sizes, medium, offset_x, offset_y, out_medium, out_index):
    span_x, span_y, _ = sizes
    fine, width = offset_x.shape[1], offset_y.shape[1]
    pairs = out_medium.shape[1]
    x, y, z = where_am_i()
    lane, row = lane_of(), row_of()
    lower = lane < half
    for m in range(2):
        for k in range(pairs):
            out_medium[m, k] = jnp.where(lower, medium[m, k], medium[m, k + pairs])

    moves = jnp.concatenate([offset_x[...].astype(jnp.float32)] * (lanes // fine), axis=1)
    moves = jnp.broadcast_to(moves, (rows, lanes))
    for r in range(2):
        place = row + r * rows
        move = jnp.sum(jnp.where(lane == place, moves, 0.0), axis=1, keepdims=True)
        target = lax.shift_right_logical(place, 1) + move.astype(jnp.int32)
        out_index[r] = jnp.clip(target, -(x * rows), (span_x - x) * rows - 1)
    coarse = lax.shift_right_logical(jnp.bitwise_and(lane, half - 1), 1) + z * (width // 2)
    move = jnp.concatenate([offset_y[...], offset_y[...]], axis=1)
    out_index[2] = coarse
    out_index[3] = jnp.clip(
        coarse + jnp.broadcast_to(move, (rows, lanes)), -(y * lanes), (span_y - y) * lanes - 1
    )


def pick(x, index, axis):
    return jnp.take_along_axis(x, index, axis=axis)


def blend_rows(plane, rim, index):
    parts = []
    for r in range(2):
        near = pick(plane, lax.shift_right_logical(row_of() + r * rows, 1), 0)
        target = index[r]
        inside = jnp.logical_and(target >= 0, target < rows)
        beyond = jnp.where(target < 0, rim[0:1], rim[1:2])
        other = jnp.where(inside, pick(plane, jnp.bitwise_and(target, rows - 1), 0), beyond)
        parts.append(0.75 * near + 0.25 * other)
    return parts


def blend_cols(inside, beside, index):
    near, target = index[2], index[3]
    at_home = jnp.logical_and(target >= 0, target < lanes)
    source = jnp.bitwise_and(target, lanes - 1)
    parts = []
    for own, other in zip(inside, beside):
        far_value = jnp.where(at_home, pick(own, source, 1), pick(other, source, 1))
        parts.append(0.75 * pick(own, near, 1) + 0.25 * far_value)
    return jnp.concatenate(parts, axis=0)


def x_scratch(packs, scratch):
    odd = flag(lax.rem(lax.axis_index("gx"), 2))
    yes = jnp.full((rows, lanes), True)

    def fill(tiles):
        for i in tiles:
            low, high = sides([pack[i] for pack in packs], odd)
            if len(packs) == 1:
                scratch[0, i] = row_terms(low, odd)
            else:
                scratch[0, i] = row_terms(low, yes)
                scratch[1, i] = row_terms(high, jnp.logical_not(yes))

    def terms(t, mask_low, mask_high):
        q = t % 4
        tile = turn(scratch[0, t // 4], -2 * q, 0)
        if len(packs) == 1:
            return jnp.where(jnp.logical_or(mask_low, mask_high), tile, 0.0)
        high = turn(scratch[1, t // 4], -2 * q, 0)
        return jnp.where(mask_low, tile, jnp.where(mask_high, high, 0.0))

    return fill, terms


def ocean_kernel(sizes, ocean, medium, *refs):
    packs = refs[:-7]
    ocean_next, ocean_rate, carry, stage_next, stage_rate, scratch, sems = refs[-7:]
    span_x, span_y, span_z = sizes
    levels, fine, _ = ocean.shape[1:]
    pairs = levels // 2
    x, y, z = where_am_i()
    x_first, x_last = one(x == 0), one(x == span_x - 1)
    joint_first = one(y == 0) * one(z == 0)
    joint_last = one(y == span_y - 1) * one(z == span_z - 1)
    row = row_of()
    low_rows = jnp.logical_and(row < 2, flag(1 - x_first))
    high_rows = jnp.logical_and(row >= rows - 2, flag(1 - x_last))
    never = jnp.full((rows, lanes), False)
    fill, terms = x_scratch(packs, scratch)
    tiles = len(ocean_x_fields) * pairs // 4
    first_tile = packs[0].shape[0] - tiles
    fill(range(first_tile, first_tile + tiles))

    def x_ends(t):
        t = 4 * first_tile + t
        return jnp.concatenate([terms(t, low_rows, never), terms(t, never, high_rows)], axis=0)

    wide = (fine, lanes)
    lower = lane_of(wide) < half
    weights_x = stencil(row_of(wide), fine, x_first, x_last)
    weights_y = stencil(
        jnp.bitwise_and(lane_of(wide), half - 1), half, joint_first, joint_last
    )
    states = [[paired_level(ocean, m, k, levels) for k in range(pairs)] for m in range(4)]

    def slope_z(m, k):
        def at(i):
            if 0 <= i < pairs:
                return states[m][i]
            return turn(states[m][i % pairs], half, 1)

        total = (at(k - 2) - at(k + 2) + 8.0 * (at(k + 1) - at(k - 1))) * (1.0 / 12.0)
        if k < 4:
            near = sum(w * at(c) for c, w in enumerate(closure_rows[k]) if w != 0.0)
            total = jnp.where(lower, near, total)
        if pairs - 1 - k < 4:
            near = sum(
                -w * at(pairs - 1 - c)
                for c, w in enumerate(closure_rows[pairs - 1 - k])
                if w != 0.0
            )
            total = jnp.where(lower, total, near)
        return total

    copies = []
    chunk = pairs // 2
    for k in range(pairs):
        bulk = jnp.concatenate([medium[0, k]] * 2, axis=0)
        light = jnp.concatenate([medium[1, k]] * 2, axis=0)
        p, u, v, w = (states[m][k] for m in range(4))
        dxu = slope(u, weights_x, 0) + x_ends(k)
        dxp = slope(p, weights_x, 0) + x_ends(pairs + k)
        dyv = slope(v, weights_y, 1)
        dyp = slope(p, weights_y, 1)
        rate_p = -bulk * (2.0 * (dxu + dyv) + slope_z(3, k)) + gravity * w / light
        rate_w = -light * slope_z(0, k)
        if k == pairs - 1:
            rate_p = rate_p + jnp.where(lower, 0.0, inv_norm * bulk * w)
        if k == 0:
            rate_w = rate_w - jnp.where(lower, inv_norm * light * p, 0.0)
        carry[0, k] = rate_p
        carry[1, k] = -2.0 * light * dyp
        carry[2, k] = p
        carry[3, k] = v
        store_pair(stage_rate, stage_next, 0, k, -2.0 * light * dxp, u)
        store_pair(stage_rate, stage_next, 1, k, rate_w, w)
        if (k + 1) % chunk == 0:
            copies += out_copies(
                ((stage_rate, ocean_rate), (stage_next, ocean_next)),
                (1, 3), k + 1 - chunk, chunk, pairs, sems, len(copies),
            )
    for copy in copies:
        copy.wait()


def store_pair(stage_rate, stage_next, slot, k, rate, state):
    pairs = stage_rate.shape[1] // 2
    rate = step_size * rate
    after = state + section_weight * rate
    stage_rate[slot, k] = rate[:, :half]
    stage_next[slot, k] = after[:, :half]
    stage_rate[slot, k + pairs] = turn(rate, half, 1)[:, :half]
    stage_next[slot, k + pairs] = turn(after, half, 1)[:, :half]


def out_copies(routes, fields, start, chunk, pairs, sems, used):
    copies = []
    for stage, out in routes:
        for slot, field in enumerate(fields):
            for base in (start, start + pairs):
                copies.append(
                    pltpu.make_async_copy(
                        stage.at[slot, pl.ds(base, chunk)],
                        out.at[field, pl.ds(base, chunk)],
                        sems.at[used + len(copies)],
                    )
                )
    run_copies(copies)
    return copies


def relay_kernel(count_x, solid, pressure, got_small, got_ya, got_yb, *refs):
    planes, out = refs[:count_x], refs[-1]
    depth = solid.shape[1]
    _, y, z = where_am_i()
    odd_y = flag(lax.rem(y, 2))
    bottom, second = flag(one(z == 0)), flag(one(z == 1))
    lane = lane_of()
    got_y = (got_ya, got_yb)
    edge_tiles = out_edge_tiles(depth)
    t = y_fields.index(2) * depth
    _, right = sides([g[t // 32] for g in got_y], odd_y)
    right = turn(right, -(4 * (t % 32) + 2), 1)
    _, right_rim = sides([g[edge_tiles + 2] for g in got_y], odd_y)
    first = lane == 0
    plane = jnp.where(first, right, solid[2, 0])
    rim = jnp.where(first, right_rim, rim_tile_of(planes))
    came = got_small[2]
    out[0] = jnp.where(bottom, plane, jnp.where(second, came, came + pressure[0]))
    out[1] = jnp.where(bottom, rim, got_small[3])
    for i in range(2):
        low, high = sides([g[edge_tiles + i] for g in got_y], odd_y)
        out[2 + i] = jnp.where(bottom, high, low)


def out_edge_tiles(depth):
    return -(-len(y_fields) * depth // 32)


def solid_kernel(sizes, solid, material, got_even, got_odd, got_ya, got_yb, *refs):
    packs = refs[:-7]
    solid_next, solid_rate, carry, stage_next, stage_rate, scratch, sems = refs[-7:]
    span_x, span_y, span_z = sizes
    depth = solid.shape[1]
    x, y, z = where_am_i()
    x_first, x_last = one(x == 0), one(x == span_x - 1)
    y_first, y_last = one(y == 0), one(y == span_y - 1)
    odd_y, odd_z = flag(lax.rem(y, 2)), flag(lax.rem(z, 2))
    lane, row = lane_of(), row_of()
    low_rows = jnp.logical_and(row < 2, flag(1 - x_first))
    high_rows = jnp.logical_and(row >= rows - 2, flag(1 - x_last))
    fill, x_terms = x_scratch(packs, scratch)
    fill(range(len(x_fields) * depth // 4))
    y_edges = []
    for i in range(out_edge_tiles(depth)):
        low, high = sides([got_ya[i], got_yb[i]], odd_y)
        y_edges.append(edge_terms(low, high, flag(1 - y_first), flag(1 - y_last)))
    end_lanes = jnp.logical_or(lane < 2, lane >= lanes - 2)

    def y_terms(t):
        return jnp.where(end_lanes, turn(y_edges[t // 32], -(4 * (t % 32) + 2), 1), 0.0)

    weights_x = stencil(row, rows, x_first, x_last)
    weights_y = stencil(lane, lanes, y_first, y_last)
    at_first, at_last = flag(one(z == 0)), flag(one(z == span_z - 1))

    def layer(i, k):
        if 0 <= k < depth:
            return solid[z_fields[i], k]
        j = 2 * i + (k + 2 if k < 0 else k - depth)
        low, high = sides([got_even[j], got_odd[j]], odd_z)
        return low if k < 0 else high

    def slope_z(i, k):
        total = (
            layer(i, k - 2) - layer(i, k + 2) + 8.0 * (layer(i, k + 1) - layer(i, k - 1))
        ) * (1.0 / 12.0)
        if k < 4:
            near = sum(w * layer(i, c) for c, w in enumerate(closure_rows[k]) if w != 0.0)
            total = jnp.where(at_first, near, total)
        if depth - 1 - k < 4:
            near = sum(
                -w * layer(i, depth - 1 - c)
                for c, w in enumerate(closure_rows[depth - 1 - k])
                if w != 0.0
            )
            total = jnp.where(at_last, near, total)
        return total

    copies = []
    for k in range(depth):
        dx = {
            m: slope(solid[m, k], weights_x, 0) + x_terms(i * depth + k, low_rows, high_rows)
            for i, m in enumerate(x_fields)
        }
        dy = {
            m: slope(solid[m, k], weights_y, 1) + y_terms(i * depth + k)
            for i, m in enumerate(y_fields)
        }
        metric = material[3, k]
        dz = {m: metric * slope_z(i, k) for i, m in enumerate(z_fields)}
        buoyancy, lame_one, lame_two = material[0, k], material[1, k], material[2, k]
        dilation = lame_one * (dx[0] + dy[1] + dz[2])
        twice = 2.0 * lame_two
        rates = [
            buoyancy * (dx[3] + dy[8] + dz[7]),
            buoyancy * (dx[8] + dy[4] + dz[6]),
            buoyancy * (dx[7] + dy[6] + dz[5]),
            dilation + twice * dx[0],
            dilation + twice * dy[1],
            dilation + twice * dz[2],
            lame_two * (dz[1] + dy[2]),
            lame_two * (dz[0] + dx[2]),
            lame_two * (dy[0] + dx[1]),
        ]
        if k == 0:
            factor = jnp.where(at_first, inv_norm * buoyancy * metric, 0.0)
            rates[0] = rates[0] + factor * solid[7, 0]
            rates[1] = rates[1] + factor * solid[6, 0]
            carry[0] = rates[2] + factor * solid[5, 0]
            carry[1] = factor
        for m, rate in enumerate(rates):
            rate = step_size * rate
            stage_rate[m, k] = rate
            stage_next[m, k] = solid[m, k] + section_weight * rate
        if k == 0:
            spans = ((0, 2, 0, 1), (3, 6, 0, 1))
        else:
            spans = ((0, 9, k, 1),) if k % 2 else ()
            spans = spans if k < 3 else ((0, 9, k - 1, 2),) if k % 2 else ()
        fresh = []
        for first, count, level, thick in spans:
            at = (pl.ds(first, count), pl.ds(level, thick))
            for stage, out in ((stage_rate, solid_rate), (stage_next, solid_next)):
                n = len(copies) + len(fresh)
                fresh.append(pltpu.make_async_copy(stage.at[at], out.at[at], sems.at[n]))
        run_copies(fresh)
        copies += fresh
    for copy in copies:
        copy.wait()


def last_kernel(
    sizes, solid, medium, pressure, index, ocean_carry, solid_carry,
    got_small, got_odd, got_far, got_ya, got_yb, *refs,
):
    _, span_y, span_z = sizes
    planes = refs[:-13]
    outs = refs[-9:-5]
    solid_next, solid_rate, ocean_next, ocean_rate = outs
    stage_next, stage_rate, vz_next, vz_rate, sems = refs[-5:]
    depth = solid.shape[1]
    pairs, fine = ocean_carry.shape[1:3]
    _, y, z = where_am_i()
    odd_y, odd_z = flag(lax.rem(y, 2)), flag(lax.rem(z, 2))
    bottom, second, top = (flag(one(z == i)) for i in (0, 1, span_z - 1))
    joint_first = one(y == 0) * one(z == 0)
    joint_last = one(y == span_y - 1) * one(z == span_z - 1)
    lane = lane_of()
    ring = 2 * len(z_fields)
    copies = []

    sum_pressure = pressure[0] + got_small[2] + got_far[0]
    rate = step_size * (solid_carry[0] + solid_carry[1] * sum_pressure)
    vz_rate[0, 0] = rate
    vz_next[0, 0] = solid[2, 0] + section_weight * rate
    at = (pl.ds(2, 1), pl.ds(0, 1))
    for stage, out in ((vz_rate, solid_rate), (vz_next, solid_next)):
        copies.append(pltpu.make_async_copy(stage, out.at[at], sems.at[len(copies)]))
    run_copies(copies)

    lows, highs = [], []
    for i in range(2):
        low, high = sides([got_small[i], got_odd[ring + i]], odd_z)
        lows.append(jnp.where(bottom, got_far[2 + i], low))
        highs.append(jnp.where(top, got_far[2 + i], high))
    has_left, has_right = flag(1 - joint_first), flag(1 - joint_last)
    outer = edge_terms(lows[1], highs[1], has_left, has_right)
    inner = edge_terms(lows[0], highs[0], has_left, has_right)
    end_lanes = jnp.logical_or(lane < 2, lane >= lanes - 2)
    mid_lanes = jnp.logical_and(lane >= half - 2, lane < half + 2)

    step = pairs // 2

    def y_ends(t, part):
        parts = []
        for r in range(fine // rows):
            q = t * (fine // rows) + r
            moved = lanes - 4 * (fine // rows) * step * part
            end = pltpu.roll(outer, jnp.bitwise_and(moved - 4 * q - 2, lanes - 1), 1)
            mid = pltpu.roll(inner, jnp.bitwise_and(moved + half - 4 * q - 2, lanes - 1), 1)
            parts.append(jnp.where(end_lanes, end, jnp.where(mid_lanes, mid, 0.0)))
        return jnp.concatenate(parts, axis=0)

    edge_tiles = out_edge_tiles(depth)
    t = y_fields.index(2) * depth
    left, _ = sides([got_ya[t // 32], got_yb[t // 32]], odd_y)
    left = turn(left, lanes - 1 - (4 * (t % 32) + 1), 1)
    left_rim, _ = sides([got_ya[edge_tiles + 2], got_yb[edge_tiles + 2]], odd_y)
    own_rim = rim_tile_of(planes)
    plane = jnp.where(bottom, solid[2, 0], jnp.where(second, got_small[2], got_far[0]))
    rim = jnp.where(bottom, own_rim, jnp.where(second, got_small[3], got_far[1]))
    beside = jnp.where(lane == 0, got_far[0], left)
    beside_rim = jnp.where(lane == 0, got_far[1], left_rim)
    bed_speed = blend_cols(
        blend_rows(plane, rim, index), blend_rows(beside, beside_rim, index), index
    )

    pull = jnp.where(lane_of((fine, lanes)) < half, 0.0, inv_norm * bed_speed)
    pull = pull * jnp.concatenate([medium[0, pairs - 1]] * 2, axis=0)
    routes = [
        (stage, out, slot, field, base)
        for stage, out in ((stage_rate, ocean_rate), (stage_next, ocean_next))
        for slot, field in enumerate((0, 2))
        for base in (0, pairs)
    ]

    def sent(part):
        return [
            pltpu.make_async_copy(
                stage.at[slot, pl.ds(base + part * step, step)],
                out.at[field, pl.ds(base + part * step, step)],
                sems.at[2 + part * len(routes) + i],
            )
            for i, (stage, out, slot, field, base) in enumerate(routes)
        ]

    def half_levels(part, _):
        for j in range(step):
            k = part * step + j
            bulk = jnp.concatenate([medium[0, k]] * 2, axis=0)
            light = jnp.concatenate([medium[1, k]] * 2, axis=0)
            rate_p = ocean_carry[0, k] - 2.0 * bulk * y_ends(j, part)
            if j == step - 1:
                rate_p = rate_p - jnp.where(part == 1, pull, 0.0)
            rate_v = ocean_carry[1, k] - 2.0 * light * y_ends(pairs + j, part)
            store_pair(stage_rate, stage_next, 0, k, rate_p, ocean_carry[2, k])
            store_pair(stage_rate, stage_next, 1, k, rate_v, ocean_carry[3, k])
        run_copies(sent(part))
        return 0

    lax.fori_loop(0, 2, half_levels, 0)
    for copy in copies + sent(0) + sent(1):
        copy.wait()


def compute(solid_state, material, ocean_state, ocean_medium, offset_x, offset_y):
    sizes = tuple(lax.axis_size(axis) for axis in ("gx", "gy", "gz"))
    span_x, span_y, span_z = sizes
    depth = solid_state.shape[1]
    levels, fine, width = ocean_state.shape[1:]
    pairs = levels // 2
    if solid_state.shape[2:] != (rows, lanes) or (fine, width) != (2 * rows, half):
        raise ValueError("tile shape")
    if depth % 4 or levels % 2 or span_z != 4 or span_x % 2 or span_y % 2 or span_y < 4:
        raise ValueError("sizes")
    f32 = jnp.float32
    vmem = pl.BlockSpec(memory_space=pltpu.VMEM)
    smem = pl.BlockSpec(memory_space=pltpu.SMEM)
    hbm = pl.BlockSpec(memory_space=pl.ANY)
    near = lambda x: pltpu.with_memory_space_constraint(x, pltpu.VMEM)
    tiles = lambda *n: pltpu.VMEM((*n, rows, lanes), f32)
    like = lambda a: jax.ShapeDtypeStruct(a.shape, f32)
    dma = pltpu.SemaphoreType.DMA
    material = near(material)
    x_rounds = pair_rounds(span_x)
    count_x = len(x_rounds)
    pack_tiles = (len(x_fields) * depth + len(ocean_x_fields) * pairs) // 4
    edge_tiles = out_edge_tiles(depth)
    layers = 2 * len(z_fields)
    solid, ocean, medium, index = pl.pallas_call(
        functools.partial(stage_kernel, sizes),
        out_shape=[
            pltpu.VMEM(solid_state.shape, f32),
            pltpu.VMEM(ocean_state.shape, f32),
            tiles(2, pairs),
            pltpu.VMEM((4, rows, lanes), jnp.int32),
        ],
        in_specs=[hbm] * 5,
        out_specs=[vmem] * 4,
        scratch_shapes=[
            pltpu.SMEM(ocean_medium.shape, f32),
            pltpu.VMEM((1, fine), jnp.int32),
            pltpu.VMEM((1, width), jnp.int32),
            dma((5,)),
        ],
        name="stage",
    )(
        solid_state,
        ocean_state,
        ocean_medium,
        offset_x.reshape(1, fine),
        offset_y.reshape(1, width),
    )
    solid, ocean = near(solid), near(ocean)
    plane = solid_state[2, 0]
    planes = [lax.ppermute(plane, "gx", p) for p in x_rounds]
    sent_x = pl.pallas_call(
        pack_x_kernel,
        out_shape=[tiles(pack_tiles) for _ in x_rounds],
        in_specs=[vmem] * 2,
        out_specs=[vmem] * count_x,
        name="pack_x",
    )(solid, ocean)
    got_x = [near(lax.ppermute(m, "gx", p)) for m, p in zip(sent_x, x_rounds)]
    sent_y, sent_small, sent_even, sent_odd, pressure = pl.pallas_call(
        pack_kernel,
        out_shape=[tiles(edge_tiles + 3), tiles(4), tiles(layers), tiles(layers + 2), tiles(1)],
        in_specs=[vmem] * 2,
        out_specs=[vmem] * 5,
        name="pack",
    )(solid, ocean)
    pressure, medium, index = map(near, (pressure, medium, index))
    ring = ("gy", "gz")
    places = [(y, z) for y in range(span_y) for z in range(span_z)]

    def over_ring(move):
        return [(y * span_z + z, y2 * span_z + z2)
                for y, z in places for y2, z2 in (move(y, z),)]

    even = over_ring(lambda y, z: (y, z ^ 1))
    inner = over_ring(
        lambda y, z: (y ^ 1, z) if z in (0, span_z - 1) else (y, z + 1 if z % 2 else z - 1)
    )
    ends = over_ring(lambda y, z: (y, span_z - 1 - z))
    rim = row_rims(planes)
    planes = [near(plane) for plane in planes]
    sent_y, sent_small = (m.at[m.shape[0] - 1, :2].set(rim) for m in (sent_y, sent_small))
    rounds_y = pair_rounds(span_y)
    got_ya = near(lax.ppermute(sent_y, "gy", rounds_y[0]))
    got_yb = near(lax.ppermute(sent_y, "gy", rounds_y[1]))
    got_y = (got_ya, got_yb)
    got_small = near(lax.ppermute(sent_small, ring, even))
    got_even = near(lax.ppermute(sent_even, ring, even))
    got_odd = near(lax.ppermute(sent_odd, ring, inner))

    ocean_next, ocean_rate, ocean_carry = pl.pallas_call(
        functools.partial(ocean_kernel, sizes),
        out_shape=[like(ocean_state), like(ocean_state), pltpu.VMEM((4, pairs, fine, lanes), f32)],
        in_specs=[vmem] * (2 + count_x),
        out_specs=[hbm, hbm, vmem],
        scratch_shapes=[
            pltpu.VMEM((2, levels, fine, width), f32),
            pltpu.VMEM((2, levels, fine, width), f32),
            pltpu.VMEM((count_x, pack_tiles, rows, lanes), f32),
            dma((16,)),
        ],
        name="ocean",
    )(ocean, medium, *got_x)

    sent_far = pl.pallas_call(
        functools.partial(relay_kernel, count_x),
        out_shape=tiles(4),
        in_specs=[vmem] * (5 + count_x),
        out_specs=vmem,
        name="relay",
    )(solid, pressure, got_small, *got_y, *planes)
    got_far = near(lax.ppermute(sent_far, ring, ends))

    solid_next, solid_rate, solid_carry = pl.pallas_call(
        functools.partial(solid_kernel, sizes),
        out_shape=[like(solid_state), like(solid_state), tiles(2)],
        in_specs=[vmem] * (6 + count_x),
        out_specs=[hbm, hbm, vmem],
        scratch_shapes=[
            pltpu.VMEM(solid_state.shape, f32),
            pltpu.VMEM(solid_state.shape, f32),
            pltpu.VMEM((count_x, pack_tiles, rows, lanes), f32),
            dma((2 * depth,)),
        ],
        name="solid",
    )(solid, material, got_even, got_odd, *got_y, *got_x)

    return pl.pallas_call(
        functools.partial(last_kernel, sizes),
        out_shape=[like(solid_state), like(solid_state), like(ocean_state), like(ocean_state)],
        in_specs=[vmem] * (11 + count_x) + [hbm] * 4,
        out_specs=[hbm] * 4,
        input_output_aliases={11 + count_x + i: i for i in range(4)},
        scratch_shapes=[
            pltpu.VMEM((2, levels, fine, width), f32),
            pltpu.VMEM((2, levels, fine, width), f32),
            tiles(1, 1),
            tiles(1, 1),
            dma((18,)),
        ],
        name="last",
    )(
        solid, medium, pressure, index, near(ocean_carry), near(solid_carry),
        got_small, got_odd, got_far, *got_y, *planes,
        solid_next, solid_rate, ocean_next, ocean_rate,
    )


def solution(mesh):
    in_specs = (
        P(None, "gz", "gx", "gy"),
        P(None, "gz", "gx", "gy"),
        P(None, None, "gx", ("gy", "gz")),
        P(),
        P("gx"),
        P(("gy", "gz")),
    )
    out_specs = (
        P(None, "gz", "gx", "gy"),
        P(None, "gz", "gx", "gy"),
        P(None, None, "gx", ("gy", "gz")),
        P(None, None, "gx", ("gy", "gz")),
    )
    return jax.shard_map(compute, mesh=mesh, in_specs=in_specs, out_specs=out_specs, check_vma=False)
```

profile of v0, /device:TPU:0, one launch (start us, length us, event | category | flops | bytes accessed | tf_op | source)
XLA Modules:
  0.0 20.4 jit_solution(2700472922348351399)
XLA Ops:
  0.6 0.7 %slice_bitcast_fusion = f32[8,128]{1,0:T(8,128)S(1)} fusion(f32[9,8,8,128]{3,2,1,0:T(8,128)} %refs_0_.1), kind=kLoop, calls=%fused_computation | loop fusion | bytes 8192 | tf_op jit(solution)/shard_map/squeeze | solution.py:719
  1.3 3.0 %collective-permute-start.3 = (f32[8,128]{1,0:T(8,128)S(1)}, f32[8,128]{1,0:T(8,128)S(1)}, u32[]{:S(2)}, u32[]{:S(2)}) collective-permute-start(f32[8,128]{1,0:T(8,128)S(1)} %slice_bitcast_fusion), channel_id=1, source_target_pairs={{0,16},{16,0},{1,17},{17,1},{2,18},{18,2},{3,19},{19,3},{4,20},{20... | collective-permute-start | bytes 12296 | tf_op jit(solution)/shard_map/ppermute | solution.py:720
  4.3 1.2 %stage.1 = (f32[9,8,8,128]{3,2,1,0:T(8,128)S(1)}, f32[4,16,16,64]{3,2,1,0:T(8,128)S(1)}, f32[2,8,8,128]{3,2,1,0:T(8,128)S(1)}, s32[4,8,128]{2,1,0:T(8,128)S(1)}) custom-call(f32[9,8,8,128]{3,2,1,0:T(8,128)} %refs_0_.1, f32[4,16,16,64]{3,2,1,0:T(8,128)} %refs_1_.1, f32[2,16]{1,0:T(2,128)} %refs_2_.1, s32[1,16]{1,0:T(1,128)} %bitcast.10, s32[1,64]{1,0:T(1,128)} %bitcast.11), custom_call_target="tpu_custom_call" | custom-call | tf_op jit(solution)/shard_map/stage/pallas_call | solution.py:694
  5.5 0.1 pack_x.1
  5.6 0.1 collective-permute-start
  5.7 0.4 %pack.1 = (f32[5,8,128]{2,1,0:T(8,128)S(1)}, f32[4,8,128]{2,1,0:T(8,128)S(1)}, f32[12,8,128]{2,1,0:T(8,128)S(1)}, f32[14,8,128]{2,1,0:T(8,128)S(1)}, f32[1,8,128]{2,1,0:T(8,128)S(1)}) custom-call(f32[9,8,8,128]{3,2,1,0:T(8,128)S(1)} %get-tuple-element.43.solid, f32[4,16,16,64]{3,2,1,0:T(8,128)S(1)} %get-tuple-element.45.ocean), custom_call_target="tpu_custom_call" | custom-call | tf_op jit(solution)/shard_map/pack/pallas_call | solution.py:729
  6.1 0.1 collective-permute-start.2
  6.2 0.0 collective-permute-done.3.refs_0_
  6.2 3.7 %collective-permute-start.6 = (f32[4,8,128]{2,1,0:T(8,128)S(1)}, f32[4,8,128]{2,1,0:T(8,128)S(1)}, u32[]{:S(2)}, u32[]{:S(2)}) collective-permute-start(f32[4,8,128]{2,1,0:T(8,128)S(1)} %get-tuple-element.60), channel_id=1, source_target_pairs={{0,1},{1,0},{2,3},{3,2},{4,5},{5,4},{6,7},{7,6},{8,9},{9,8},{10,11... | collective-permute-start | bytes 49160 | tf_op jit(solution)/shard_map/ppermute | solution.py:756
  9.9 0.1 collective-permute-start.1
  10.0 0.0 collective-permute-start.5
  10.0 1.8 %collective-permute-done.6.got_small = f32[4,8,128]{2,1,0:T(8,128)S(1)} collective-permute-done((f32[4,8,128]{2,1,0:T(8,128)S(1)}, f32[4,8,128]{2,1,0:T(8,128)S(1)}, u32[]{:S(2)}, u32[]{:S(2)}) %collective-permute-start.6) | collective-permute-done | bytes 16416 | tf_op jit(solution)/shard_map/ppermute | solution.py:756
  11.8 0.0 collective-permute-start.4
  11.8 1.5 %collective-permute-done.5.got_yb = f32[5,8,128]{2,1,0:T(8,128)S(1)} collective-permute-done((f32[5,8,128]{2,1,0:T(8,128)S(1)}, f32[5,8,128]{2,1,0:T(8,128)S(1)}, u32[]{:S(2)}, u32[]{:S(2)}) %collective-permute-start.5) | collective-permute-done | bytes 20512 | tf_op jit(solution)/shard_map/ppermute | solution.py:754
  13.4 0.0 collective-permute-done.4.got_ya
  13.4 0.1 relay.1
  13.4 2.4 %collective-permute-start.7 = (f32[4,8,128]{2,1,0:T(8,128)S(1)}, f32[4,8,128]{2,1,0:T(8,128)S(1)}, u32[]{:S(2)}, u32[]{:S(2)}) collective-permute-start(f32[4,8,128]{2,1,0:T(8,128)S(1)} %relay.1), channel_id=1, source_target_pairs={{0,3},{1,2},{2,1},{3,0},{4,7},{5,6},{6,5},{7,4},{8,11},{9,10},{10,... | collective-permute-start | bytes 49160 | tf_op jit(solution)/shard_map/ppermute | solution.py:781
  15.9 0.0 collective-permute-done.refs_0_
  15.9 0.0 copy-start
  15.9 1.3 %ocean.1 = (f32[4,16,16,64]{3,2,1,0:T(8,128)}, f32[4,16,16,64]{3,2,1,0:T(8,128)}, f32[4,8,16,128]{3,2,1,0:T(8,128)S(1)}) custom-call(f32[4,16,16,64]{3,2,1,0:T(8,128)S(1)} %get-tuple-element.45.ocean, f32[2,8,8,128]{3,2,1,0:T(8,128)S(1)} %get-tuple-element.44.medium, f32[16,8,128]{2,1,0:T(8,128)S(1)} %collective-permute-done.refs_0_), custom_call_target="tpu_custom_call" | custom-call | tf_op jit(solution)/shard_map/ocean/pallas_call | solution.py:760
  17.2 0.0 collective-permute-done.1.got_even
  17.2 0.0 collective-permute-done.2.got_odd
  17.2 0.0 copy-done
  17.2 1.3 %solid.1 = (f32[9,8,8,128]{3,2,1,0:T(8,128)}, f32[9,8,8,128]{3,2,1,0:T(8,128)}, f32[2,8,128]{2,1,0:T(8,128)S(1)}) custom-call(f32[9,8,8,128]{3,2,1,0:T(8,128)S(1)} %get-tuple-element.43.solid, f32[4,8,8,128]{3,2,1,0:T(8,128)S(1)} %copy-done, f32[12,8,128]{2,1,0:T(8,128)S(1)} %collective-permute-done.1.got_even, ...), custom_call_target="tpu_custom_call" | custom-call | tf_op jit(solution)/shard_map/solid/pallas_call | solution.py:783
  18.5 0.4 %collective-permute-done.7.got_far = f32[4,8,128]{2,1,0:T(8,128)S(1)} collective-permute-done((f32[4,8,128]{2,1,0:T(8,128)S(1)}, f32[4,8,128]{2,1,0:T(8,128)S(1)}, u32[]{:S(2)}, u32[]{:S(2)}) %collective-permute-start.7) | collective-permute-done | bytes 16416 | tf_op jit(solution)/shard_map/ppermute | solution.py:781
  19.0 1.4 %last.1 = (f32[9,8,8,128]{3,2,1,0:T(8,128)}, f32[9,8,8,128]{3,2,1,0:T(8,128)}, f32[4,16,16,64]{3,2,1,0:T(8,128)}, f32[4,16,16,64]{3,2,1,0:T(8,128)}) custom-call(f32[9,8,8,128]{3,2,1,0:T(8,128)S(1)} %get-tuple-element.43.solid, ...), custom_call_target="tpu_custom_call", output_to_operand_aliasing={{0}: (12, {}), {1}: (13, {}), {2}: (14, {}), {3}: (15, {})} | custom-call | tf_op jit(solution)/shard_map/last/pallas_call | solution.py:797
  (2 shorter events, 0.0 us)
Async XLA Ops:
  1.3 4.9 %collective-permute-start.3 = (f32[8,128]{1,0:T(8,128)S(1)}, f32[8,128]{1,0:T(8,128)S(1)}, u32[]{:S(2)}, u32[]{:S(2)}) collective-permute-start(f32[8,128]{1,0:T(8,128)S(1)} %slice_bitcast_fusion), channel_id=1, source_target_pairs={{0,16},{16,0},{1,17},{17,1},{2,18},{18,2},{3,19},{19,3},{4,20},{20... | collective-permute-start | bytes 12296 | tf_op jit(solution)/shard_map/ppermute | solution.py:720
  5.6 10.3 %collective-permute-start = (f32[16,8,128]{2,1,0:T(8,128)S(1)}, f32[16,8,128]{2,1,0:T(8,128)S(1)}, u32[]{:S(2)}, u32[]{:S(2)}) collective-permute-start(f32[16,8,128]{2,1,0:T(8,128)S(1)} %pack_x.1), channel_id=1, source_target_pairs={{0,16},{16,0},{1,17},{17,1},{2,18},{18,2},{3,19},{19,3},{4,20},{20... | collective-permute-start | bytes 196616 | tf_op jit(solution)/shard_map/ppermute | solution.py:728
  6.1 11.1 %collective-permute-start.2 = (f32[14,8,128]{2,1,0:T(8,128)S(1)}, f32[14,8,128]{2,1,0:T(8,128)S(1)}, u32[]{:S(2)}, u32[]{:S(2)}) collective-permute-start(f32[14,8,128]{2,1,0:T(8,128)S(1)} %get-tuple-element.50), channel_id=1, source_target_pairs={{0,4},{1,2},{2,1},{3,7},{4,0},{5,6},{6,5},{7,3},{8,12},{9,10},{10,... | collective-permute-start | bytes 172040 | tf_op jit(solution)/shard_map/ppermute | solution.py:758
  6.2 5.6 %collective-permute-start.6 = (f32[4,8,128]{2,1,0:T(8,128)S(1)}, f32[4,8,128]{2,1,0:T(8,128)S(1)}, u32[]{:S(2)}, u32[]{:S(2)}) collective-permute-start(f32[4,8,128]{2,1,0:T(8,128)S(1)} %get-tuple-element.60), channel_id=1, source_target_pairs={{0,1},{1,0},{2,3},{3,2},{4,5},{5,4},{6,7},{7,6},{8,9},{9,8},{10,11... | collective-permute-start | bytes 49160 | tf_op jit(solution)/shard_map/ppermute | solution.py:756
  9.9 7.3 %collective-permute-start.1 = (f32[12,8,128]{2,1,0:T(8,128)S(1)}, f32[12,8,128]{2,1,0:T(8,128)S(1)}, u32[]{:S(2)}, u32[]{:S(2)}) collective-permute-start(f32[12,8,128]{2,1,0:T(8,128)S(1)} %get-tuple-element.49), channel_id=1, source_target_pairs={{0,1},{1,0},{2,3},{3,2},{4,5},{5,4},{6,7},{7,6},{8,9},{9,8},{10,11... | collective-permute-start | bytes 147464 | tf_op jit(solution)/shard_map/ppermute | solution.py:757
  10.0 3.4 %collective-permute-start.5 = (f32[5,8,128]{2,1,0:T(8,128)S(1)}, f32[5,8,128]{2,1,0:T(8,128)S(1)}, u32[]{:S(2)}, u32[]{:S(2)}) collective-permute-start(f32[5,8,128]{2,1,0:T(8,128)S(1)} %get-tuple-element.61), channel_id=1, source_target_pairs={{0,12},{4,8},{8,4},{12,0},{1,13},{5,9},{9,5},{13,1},{2,14},{6,10},... | collective-permute-start | bytes 61448 | tf_op jit(solution)/shard_map/ppermute | solution.py:754
  11.8 1.5 %collective-permute-start.4 = (f32[5,8,128]{2,1,0:T(8,128)S(1)}, f32[5,8,128]{2,1,0:T(8,128)S(1)}, u32[]{:S(2)}, u32[]{:S(2)}) collective-permute-start(f32[5,8,128]{2,1,0:T(8,128)S(1)} %get-tuple-element.61), channel_id=1, source_target_pairs={{0,4},{4,0},{8,12},{12,8},{1,5},{5,1},{9,13},{13,9},{2,6},{6,2},{1... | collective-permute-start | bytes 61448 | tf_op jit(solution)/shard_map/ppermute | solution.py:753
  13.4 5.5 %collective-permute-start.7 = (f32[4,8,128]{2,1,0:T(8,128)S(1)}, f32[4,8,128]{2,1,0:T(8,128)S(1)}, u32[]{:S(2)}, u32[]{:S(2)}) collective-permute-start(f32[4,8,128]{2,1,0:T(8,128)S(1)} %relay.1), channel_id=1, source_target_pairs={{0,3},{1,2},{2,1},{3,0},{4,7},{5,6},{6,5},{7,4},{8,11},{9,10},{10,... | collective-permute-start | bytes 49160 | tf_op jit(solution)/shard_map/ppermute | solution.py:781
  15.9 1.4 %copy-start = (f32[4,8,8,128]{3,2,1,0:T(8,128)S(1)}, f32[4,8,8,128]{3,2,1,0:T(8,128)}, u32[]{:S(2)}) copy-start(f32[4,8,8,128]{3,2,1,0:T(8,128)} %material.1) | copy-start | bytes 393220
where the time goes:
time: 20.6 us; the launch traced here: 20.4 us
  starting transfers between devices  9.31 us (45%)
  Pallas kernels  5.8 us (28%)
  waiting for transfers between devices  3.81 us (18%)
  between operations  0.73 us (4%)
  local copies, waits for them, and re-layouts  0.7 us (3%)
    ppermute x1, starting transfers between devices, compute(): got_small = near(lax.ppermute(sent_small, ring, even))  3.7 us
    ppermute x1, starting transfers between devices, compute(): planes = [lax.ppermute(plane, 'gx', p) for p in x_rounds]  2.97 us
    ppermute x1, starting transfers between devices, compute(): got_far = near(lax.ppermute(sent_far, ring, ends))  2.41 us
    ppermute x1, waiting for transfers between devices, compute(): got_small = near(lax.ppermute(sent_small, ring, even))  1.81 us
    ppermute x1, waiting for transfers between devices, compute(): got_yb = near(lax.ppermute(sent_y, 'gy', rounds_y[1]))  1.54 us
    pallas_call x1, Pallas kernels, compute(): pl.pallas_call(functools.partial(last_kernel, sizes), out_shape=[like(sol...  1.37 us
    pallas_call x1, Pallas kernels, compute(): pl.pallas_call(functools.partial(ocean_kernel, sizes), out_shape=[like(oc...  1.34 us
    pallas_call x1, Pallas kernels, compute(): pl.pallas_call(functools.partial(solid_kernel, sizes), out_shape=[like(so...  1.3 us
  transfers between devices with their start and end apart: 8, of which 3 were waited for; matrix products, arithmetic and copies ran while one was open for 0% of the time, Pallas kernels for 22%

commit v1 on v0

--- a/solution.py
+++ b/solution.py
@@ -70,13 +70,13 @@
     return total
 
 
-def pack_edges(tiles):
+def pack_edges(tiles, offset=2):
     group = lax.shift_right_logical(lane_of(), 2)
     out = []
     for start in range(0, len(tiles), 32):
         acc = jnp.zeros((rows, lanes), jnp.float32)
         for q, tile in enumerate(tiles[start : start + 32]):
-            acc = jnp.where(group == q, turn(tile, 4 * q + 2, 1), acc)
+            acc = jnp.where(group == q, turn(tile, 4 * q + offset, 1), acc)
         out.append(acc)
     return out
 
@@ -150,10 +150,9 @@
         copy.start()
 
 
-def stage_kernel(sizes, *refs):
+def stage_kernel(*refs):
     solid_far, ocean_far, medium_far, offset_x_far, offset_y_far = refs[:5]
-    solid, ocean, medium, index = refs[5:9]
-    small, offset_x, offset_y, sems = refs[9:]
+    solid, ocean, small, offset_x, offset_y, sems = refs[5:]
     copies = [
         pltpu.make_async_copy(solid_far, solid, sems.at[0]),
         pltpu.make_async_copy(ocean_far, ocean, sems.at[1]),
@@ -162,10 +161,7 @@
         pltpu.make_async_copy(offset_y_far, offset_y, sems.at[4]),
     ]
     run_copies(copies)
-    for copy in copies[2:]:
-        copy.wait()
-    fill_tables(sizes, small, offset_x, offset_y, medium, index)
-    for copy in copies[:2]:
+    for copy in copies:
         copy.wait()
 
 
@@ -201,35 +197,22 @@
     emit(heads, base)
 
 
-def pack_kernel(solid, ocean, out_y, out_small, out_even, out_odd, out_pressure):
+def pack_kernel(solid, ocean, out_y, out_small, out_pressure):
     levels, fine, width = ocean.shape[1:]
     depth = solid.shape[1]
     _, _, z = where_am_i()
-    odd_z = lax.rem(z, 2)
     zero = jnp.zeros((rows, lanes), jnp.float32)
     packed = pack_edges([solid[field, k] for field in y_fields for k in range(depth)])
-    outer, inner = [], []
+    tiles = []
     for field in ocean_y_fields:
         for k in range(levels // 2):
             tile = paired_level(ocean, field, k, levels)
-            for r in range(0, fine, rows):
-                outer.append(tile[r : r + rows])
-                inner.append(turn(tile[r : r + rows], half, 1))
-    ends = pack_edges(outer) + pack_edges(inner)
+            tiles += [tile[r : r + rows] for r in range(0, fine, rows)]
+    ends = pack_edges(tiles) + pack_edges(tiles, half + 2)
     for i, tile in enumerate(packed + ends + [zero]):
         out_y[i] = tile
-    start_even = (1 - odd_z) * (depth - 2)
-    start_odd = odd_z * (depth - 2)
-    count = 0
-    for field in z_fields:
-        for k in range(2):
-            out_even[count] = solid[field, start_even + k]
-            out_odd[count] = solid[field, start_odd + k]
-            count += 1
     for i, tile in enumerate(ends):
         out_small[i] = tile
-        out_odd[count + i] = tile
-
     deepest = ocean[0, levels - 1]
     deepest = jnp.concatenate([deepest, deepest], axis=1)
     source = jnp.bitwise_and(2 * row_of(), rows - 1)
@@ -248,6 +231,22 @@
     out_small[3] = zero
 
 
+def pack_z_kernel(
+    sizes, solid, sent_small, medium, offset_x, offset_y, out_even, out_odd, out_medium, out_index
+):
+    fill_tables(sizes, medium, offset_x, offset_y, out_medium, out_index)
+    odd_z = lax.rem(lax.axis_index("gz"), 2)
+    depth = solid.shape[1]
+    start_even = (1 - odd_z) * (depth - 2)
+    start_odd = odd_z * (depth - 2)
+    for i, field in enumerate(z_fields):
+        for k in range(2):
+            out_even[2 * i + k] = solid[field, start_even + k]
+            out_odd[2 * i + k] = solid[field, start_odd + k]
+    for i in range(2):
+        out_odd[2 * len(z_fields) + i] = sent_small[i]
+
+
 def fill_tables(sizes, medium, offset_x, offset_y, out_medium, out_index):
     span_x, span_y, _ = sizes
     fine, width = offset_x.shape[1], offset_y.shape[1]
@@ -256,8 +255,10 @@
     lane, row = lane_of(), row_of()
     lower = lane < half
     for m in range(2):
+        values = jnp.concatenate([medium[m : m + 1, :]] * (lanes // (2 * pairs)), axis=1)
+        values = jnp.broadcast_to(values, (rows, lanes))
         for k in range(pairs):
-            out_medium[m, k] = jnp.where(lower, medium[m, k], medium[m, k + pairs])
+            out_medium[m, k] = pick(values, jnp.where(lower, k, k + pairs), 1)
 
     moves = jnp.concatenate([offset_x[...].astype(jnp.float32)] * (lanes // fine), axis=1)
     moves = jnp.broadcast_to(moves, (rows, lanes))
@@ -603,15 +604,12 @@
     end_lanes = jnp.logical_or(lane < 2, lane >= lanes - 2)
     mid_lanes = jnp.logical_and(lane >= half - 2, lane < half + 2)
 
-    step = pairs // 2
-
-    def y_ends(t, part):
+    def y_ends(t):
         parts = []
         for r in range(fine // rows):
             q = t * (fine // rows) + r
-            moved = lanes - 4 * (fine // rows) * step * part
-            end = pltpu.roll(outer, jnp.bitwise_and(moved - 4 * q - 2, lanes - 1), 1)
-            mid = pltpu.roll(inner, jnp.bitwise_and(moved + half - 4 * q - 2, lanes - 1), 1)
+            end = turn(outer, -4 * q - 2, 1)
+            mid = turn(inner, half - 4 * q - 2, 1)
             parts.append(jnp.where(end_lanes, end, jnp.where(mid_lanes, mid, 0.0)))
         return jnp.concatenate(parts, axis=0)
 
@@ -631,39 +629,23 @@
 
     pull = jnp.where(lane_of((fine, lanes)) < half, 0.0, inv_norm * bed_speed)
     pull = pull * jnp.concatenate([medium[0, pairs - 1]] * 2, axis=0)
-    routes = [
-        (stage, out, slot, field, base)
-        for stage, out in ((stage_rate, ocean_rate), (stage_next, ocean_next))
-        for slot, field in enumerate((0, 2))
-        for base in (0, pairs)
-    ]
-
-    def sent(part):
-        return [
-            pltpu.make_async_copy(
-                stage.at[slot, pl.ds(base + part * step, step)],
-                out.at[field, pl.ds(base + part * step, step)],
-                sems.at[2 + part * len(routes) + i],
+    for slot, field in ((1, 2), (0, 0)):
+        for k in range(pairs):
+            scale = jnp.concatenate([medium[slot, k]] * 2, axis=0)
+            ends = y_ends((pairs if slot else 0) + k)
+            rate = ocean_carry[slot, k] - 2.0 * scale * ends
+            if slot == 0 and k == pairs - 1:
+                rate = rate - pull
+            store_pair(stage_rate, stage_next, slot, k, rate, ocean_carry[2 + slot, k])
+        fresh = [
+            pltpu.make_async_copy(stage.at[slot], out.at[field], sems.at[len(copies) + i])
+            for i, (stage, out) in enumerate(
+                ((stage_rate, ocean_rate), (stage_next, ocean_next))
             )
-            for i, (stage, out, slot, field, base) in enumerate(routes)
         ]
-
-    def half_levels(part, _):
-        for j in range(step):
-            k = part * step + j
-            bulk = jnp.concatenate([medium[0, k]] * 2, axis=0)
-            light = jnp.concatenate([medium[1, k]] * 2, axis=0)
-            rate_p = ocean_carry[0, k] - 2.0 * bulk * y_ends(j, part)
-            if j == step - 1:
-                rate_p = rate_p - jnp.where(part == 1, pull, 0.0)
-            rate_v = ocean_carry[1, k] - 2.0 * light * y_ends(pairs + j, part)
-            store_pair(stage_rate, stage_next, 0, k, rate_p, ocean_carry[2, k])
-            store_pair(stage_rate, stage_next, 1, k, rate_v, ocean_carry[3, k])
-        run_copies(sent(part))
-        return 0
-
-    lax.fori_loop(0, 2, half_levels, 0)
-    for copy in copies + sent(0) + sent(1):
+        run_copies(fresh)
+        copies += fresh
+    for copy in copies:
         copy.wait()
 
 
@@ -691,22 +673,18 @@
     pack_tiles = (len(x_fields) * depth + len(ocean_x_fields) * pairs) // 4
     edge_tiles = out_edge_tiles(depth)
     layers = 2 * len(z_fields)
-    solid, ocean, medium, index = pl.pallas_call(
-        functools.partial(stage_kernel, sizes),
+    solid, ocean, small, move_x, move_y = pl.pallas_call(
+        stage_kernel,
         out_shape=[
             pltpu.VMEM(solid_state.shape, f32),
             pltpu.VMEM(ocean_state.shape, f32),
-            tiles(2, pairs),
-            pltpu.VMEM((4, rows, lanes), jnp.int32),
+            pltpu.VMEM(ocean_medium.shape, f32),
+            pltpu.VMEM((1, fine), jnp.int32),
+            pltpu.VMEM((1, width), jnp.int32),
         ],
         in_specs=[hbm] * 5,
-        out_specs=[vmem] * 4,
-        scratch_shapes=[
-            pltpu.SMEM(ocean_medium.shape, f32),
-            pltpu.VMEM((1, fine), jnp.int32),
-            pltpu.VMEM((1, width), jnp.int32),
-            dma((5,)),
-        ],
+        out_specs=[vmem] * 5,
+        scratch_shapes=[dma((5,))],
         name="stage",
     )(
         solid_state,
@@ -726,14 +704,14 @@
         name="pack_x",
     )(solid, ocean)
     got_x = [near(lax.ppermute(m, "gx", p)) for m, p in zip(sent_x, x_rounds)]
-    sent_y, sent_small, sent_even, sent_odd, pressure = pl.pallas_call(
+    sent_y, sent_small, pressure = pl.pallas_call(
         pack_kernel,
-        out_shape=[tiles(edge_tiles + 3), tiles(4), tiles(layers), tiles(layers + 2), tiles(1)],
+        out_shape=[tiles(edge_tiles + 3), tiles(4), tiles(1)],
         in_specs=[vmem] * 2,
-        out_specs=[vmem] * 5,
+        out_specs=[vmem] * 3,
         name="pack",
     )(solid, ocean)
-    pressure, medium, index = map(near, (pressure, medium, index))
+    pressure = near(pressure)
     ring = ("gy", "gz")
     places = [(y, z) for y in range(span_y) for z in range(span_z)]
 
@@ -749,6 +727,19 @@
     rim = row_rims(planes)
     planes = [near(plane) for plane in planes]
     sent_y, sent_small = (m.at[m.shape[0] - 1, :2].set(rim) for m in (sent_y, sent_small))
+    sent_even, sent_odd, medium, index = pl.pallas_call(
+        functools.partial(pack_z_kernel, sizes),
+        out_shape=[
+            tiles(layers),
+            tiles(layers + 2),
+            tiles(2, pairs),
+            pltpu.VMEM((4, rows, lanes), jnp.int32),
+        ],
+        in_specs=[vmem] * 5,
+        out_specs=[vmem] * 4,
+        name="pack_z",
+    )(solid, near(sent_small), near(small), near(move_x), near(move_y))
+    medium, index = near(medium), near(index)
     rounds_y = pair_rounds(span_y)
     got_ya = near(lax.ppermute(sent_y, "gy", rounds_y[0]))
     got_yb = near(lax.ppermute(sent_y, "gy", rounds_y[1]))
@@ -805,7 +796,7 @@
             pltpu.VMEM((2, levels, fine, width), f32),
             tiles(1, 1),
             tiles(1, 1),
-            dma((18,)),
+            dma((6,)),
         ],
         name="last",
     )(

time: 20.6 us -> 20.2 us (0.981)
  Pallas kernels: 5.8 us -> 5.57 us
    pallas_call x1, Pallas kernels: 1.37 us -> 1.1 us  [compute(): pl.pallas_call(functools.partial(last_kernel, sizes), out_shape=[like(sol...]
    pallas_call x1 -> x2, Pallas kernels: 1.18 us -> 1.4 us  [the longest x1 1.18 us: compute(): pl.pallas_call(stage_kernel, out_shape=[pltpu.VMEM(solid_state.shape, f32...]
where the time goes in v1:
time: 20.2 us; the launch traced here: 20 us
  starting transfers between devices  9.33 us (46%)
  Pallas kernels  5.57 us (28%)
  waiting for transfers between devices  3.68 us (18%)
  between operations  0.73 us (4%)
  local copies, waits for them, and re-layouts  0.7 us (3%)
    ppermute x1, starting transfers between devices, compute(): got_small = near(lax.ppermute(sent_small, ring, even))  3.66 us
    ppermute x1, starting transfers between devices, compute(): planes = [lax.ppermute(plane, 'gx', p) for p in x_rounds]  2.97 us
    ppermute x1, starting transfers between devices, compute(): got_far = near(lax.ppermute(sent_far, ring, ends))  2.54 us
    ppermute x1, waiting for transfers between devices, compute(): got_small = near(lax.ppermute(sent_small, ring, even))  1.86 us
    ppermute x1, waiting for transfers between devices, compute(): got_yb = near(lax.ppermute(sent_y, 'gy', rounds_y[1]))  1.49 us
    pallas_call x1, Pallas kernels, compute(): pl.pallas_call(functools.partial(ocean_kernel, sizes), out_shape=[like(oc...  1.34 us
    pallas_call x1, Pallas kernels, compute(): pl.pallas_call(functools.partial(solid_kernel, sizes), out_shape=[like(so...  1.3 us
    pallas_call x1, Pallas kernels, compute(): pl.pallas_call(stage_kernel, out_shape=[pltpu.VMEM(solid_state.shape, f32...  1.18 us
  transfers between devices with their start and end apart: 8, of which 3 were waited for; matrix products, arithmetic and copies ran while one was open for 0% of the time, Pallas kernels for 22%

profile of v1, /device:TPU:0, one launch (start us, length us, event | category | flops | bytes accessed | tf_op | source)
XLA Modules:
  0.0 20.0 jit_solution(11634230489317377069)
XLA Ops:
  0.6 0.7 %slice_bitcast_fusion = f32[8,128]{1,0:T(8,128)S(1)} fusion(f32[9,8,8,128]{3,2,1,0:T(8,128)} %refs_0_.1), kind=kLoop, calls=%fused_computation | loop fusion | bytes 8192 | tf_op jit(solution)/shard_map/squeeze | solution.py:697
  1.3 3.0 %collective-permute-start = (f32[8,128]{1,0:T(8,128)S(1)}, f32[8,128]{1,0:T(8,128)S(1)}, u32[]{:S(2)}, u32[]{:S(2)}) collective-permute-start(f32[8,128]{1,0:T(8,128)S(1)} %slice_bitcast_fusion), channel_id=1, source_target_pairs={{0,16},{16,0},{1,17},{17,1},{2,18},{18,2},{3,19},{19,3},{4,20},{20... | collective-permute-start | bytes 12296 | tf_op jit(solution)/shard_map/ppermute | solution.py:698
  4.3 1.2 %stage.1 = (f32[9,8,8,128]{3,2,1,0:T(8,128)S(1)}, f32[4,16,16,64]{3,2,1,0:T(8,128)S(1)}, f32[2,16]{1,0:T(2,128)S(1)}, s32[1,16]{1,0:T(1,128)S(1)}, s32[1,64]{1,0:T(1,128)S(1)}) custom-call(f32[9,8,8,128]{3,2,1,0:T(8,128)} %refs_0_.1, f32[4,16,16,64]{3,2,1,0:T(8,128)} %refs_1_.1, f32[2,16]{1,0:T(2,128)} %refs_2_.1, s32[1,16]{1,0:T(1,128)} %bitcast.10, ...), custom_call_target="tpu_custom_call" | custom-call | tf_op jit(solution)/shard_map/stage/pallas_call | solution.py:676
  5.5 0.1 pack_x.1
  5.6 0.1 collective-permute-start.1
  5.7 0.3 %pack.1 = (f32[5,8,128]{2,1,0:T(8,128)S(1)}, f32[4,8,128]{2,1,0:T(8,128)S(1)}, f32[1,8,128]{2,1,0:T(8,128)S(1)}) custom-call(f32[9,8,8,128]{3,2,1,0:T(8,128)S(1)} %get-tuple-element.46.solid, f32[4,16,16,64]{3,2,1,0:T(8,128)S(1)} %get-tuple-element.47.ocean), custom_call_target="tpu_custom_call" | custom-call | tf_op jit(solution)/shard_map/pack/pallas_call | solution.py:707
  5.9 0.0 collective-permute-done.refs_0_
  6.0 0.2 %pack_z.1 = (f32[12,8,128]{2,1,0:T(8,128)S(1)}, f32[14,8,128]{2,1,0:T(8,128)S(1)}, f32[2,8,8,128]{3,2,1,0:T(8,128)S(1)}, s32[4,8,128]{2,1,0:T(8,128)S(1)}) custom-call(f32[9,8,8,128]{3,2,1,0:T(8,128)S(1)} %get-tuple-element.46.solid, f32[4,8,128]{2,1,0:T(8,128)S(1)} %get-tuple-element.67.sent_small, f32[2,16]{1,0:T(2,128)S(1)} %get-tuple-element.49.medium, ...), custom_call_target="tpu_custom_call" | custom-call | tf_op jit(solution)/shard_map/pack_z/pallas_call | solution.py:730
  6.2 0.1 collective-permute-start.3
  6.3 3.7 %collective-permute-start.6 = (f32[4,8,128]{2,1,0:T(8,128)S(1)}, f32[4,8,128]{2,1,0:T(8,128)S(1)}, u32[]{:S(2)}, u32[]{:S(2)}) collective-permute-start(f32[4,8,128]{2,1,0:T(8,128)S(1)} %get-tuple-element.67.sent_small), channel_id=1, source_target_pairs={{0,1},{1,0},{2,3},{3,2},{4,5},{5,4},{6,7},{7,6},{8,9},{9,8},{10,11... | collective-permute-start | bytes 49160 | tf_op jit(solution)/shard_map/ppermute | solution.py:747
  9.9 0.0 collective-permute-start.2
  9.9 0.0 collective-permute-start.5
  10.0 1.9 %collective-permute-done.6.got_small = f32[4,8,128]{2,1,0:T(8,128)S(1)} collective-permute-done((f32[4,8,128]{2,1,0:T(8,128)S(1)}, f32[4,8,128]{2,1,0:T(8,128)S(1)}, u32[]{:S(2)}, u32[]{:S(2)}) %collective-permute-start.6) | collective-permute-done | bytes 16416 | tf_op jit(solution)/shard_map/ppermute | solution.py:747
  11.8 0.0 collective-permute-start.4
  11.8 1.5 %collective-permute-done.5.got_yb = f32[5,8,128]{2,1,0:T(8,128)S(1)} collective-permute-done((f32[5,8,128]{2,1,0:T(8,128)S(1)}, f32[5,8,128]{2,1,0:T(8,128)S(1)}, u32[]{:S(2)}, u32[]{:S(2)}) %collective-permute-start.5) | collective-permute-done | bytes 20512 | tf_op jit(solution)/shard_map/ppermute | solution.py:745
  13.3 0.0 collective-permute-done.4.got_ya
  13.3 0.1 relay.1
  13.4 2.5 %collective-permute-start.7 = (f32[4,8,128]{2,1,0:T(8,128)S(1)}, f32[4,8,128]{2,1,0:T(8,128)S(1)}, u32[]{:S(2)}, u32[]{:S(2)}) collective-permute-start(f32[4,8,128]{2,1,0:T(8,128)S(1)} %relay.1), channel_id=1, source_target_pairs={{0,3},{1,2},{2,1},{3,0},{4,7},{5,6},{6,5},{7,4},{8,11},{9,10},{10,... | collective-permute-start | bytes 49160 | tf_op jit(solution)/shard_map/ppermute | solution.py:772
  15.9 0.0 collective-permute-done.1.refs_0_
  15.9 0.0 copy-start
  15.9 1.3 %ocean.1 = (f32[4,16,16,64]{3,2,1,0:T(8,128)}, f32[4,16,16,64]{3,2,1,0:T(8,128)}, f32[4,8,16,128]{3,2,1,0:T(8,128)S(1)}) custom-call(f32[4,16,16,64]{3,2,1,0:T(8,128)S(1)} %get-tuple-element.47.ocean, f32[2,8,8,128]{3,2,1,0:T(8,128)S(1)} %get-tuple-element.52.medium, f32[16,8,128]{2,1,0:T(8,128)S(1)} %collective-permute-done.1.refs_0_), custom_call_target="tpu_custom_call" | custom-call | tf_op jit(solution)/shard_map/ocean/pallas_call | solution.py:751
  17.3 0.0 collective-permute-done.2.got_even
  17.3 0.0 collective-permute-done.3.got_odd
  17.3 0.0 copy-done
  17.3 1.3 %solid.1 = (f32[9,8,8,128]{3,2,1,0:T(8,128)}, f32[9,8,8,128]{3,2,1,0:T(8,128)}, f32[2,8,128]{2,1,0:T(8,128)S(1)}) custom-call(f32[9,8,8,128]{3,2,1,0:T(8,128)S(1)} %get-tuple-element.46.solid, f32[4,8,8,128]{3,2,1,0:T(8,128)S(1)} %copy-done, f32[12,8,128]{2,1,0:T(8,128)S(1)} %collective-permute-done.2.got_even, ...), custom_call_target="tpu_custom_call" | custom-call | tf_op jit(solution)/shard_map/solid/pallas_call | solution.py:774
  18.6 0.3 %collective-permute-done.7.got_far = f32[4,8,128]{2,1,0:T(8,128)S(1)} collective-permute-done((f32[4,8,128]{2,1,0:T(8,128)S(1)}, f32[4,8,128]{2,1,0:T(8,128)S(1)}, u32[]{:S(2)}, u32[]{:S(2)}) %collective-permute-start.7) | collective-permute-done | bytes 16416 | tf_op jit(solution)/shard_map/ppermute | solution.py:772
  18.9 1.1 %last.1 = (f32[9,8,8,128]{3,2,1,0:T(8,128)}, f32[9,8,8,128]{3,2,1,0:T(8,128)}, f32[4,16,16,64]{3,2,1,0:T(8,128)}, f32[4,16,16,64]{3,2,1,0:T(8,128)}) custom-call(f32[9,8,8,128]{3,2,1,0:T(8,128)S(1)} %get-tuple-element.46.solid, ...), custom_call_target="tpu_custom_call", output_to_operand_aliasing={{0}: (12, {}), {1}: (13, {}), {2}: (14, {}), {3}: (15, {})} | custom-call | tf_op jit(solution)/shard_map/last/pallas_call | solution.py:788
  (2 shorter events, 0.0 us)
Async XLA Ops:
  1.3 4.6 %collective-permute-start = (f32[8,128]{1,0:T(8,128)S(1)}, f32[8,128]{1,0:T(8,128)S(1)}, u32[]{:S(2)}, u32[]{:S(2)}) collective-permute-start(f32[8,128]{1,0:T(8,128)S(1)} %slice_bitcast_fusion), channel_id=1, source_target_pairs={{0,16},{16,0},{1,17},{17,1},{2,18},{18,2},{3,19},{19,3},{4,20},{20... | collective-permute-start | bytes 12296 | tf_op jit(solution)/shard_map/ppermute | solution.py:698
  5.6 10.3 %collective-permute-start.1 = (f32[16,8,128]{2,1,0:T(8,128)S(1)}, f32[16,8,128]{2,1,0:T(8,128)S(1)}, u32[]{:S(2)}, u32[]{:S(2)}) collective-permute-start(f32[16,8,128]{2,1,0:T(8,128)S(1)} %pack_x.1), channel_id=1, source_target_pairs={{0,16},{16,0},{1,17},{17,1},{2,18},{18,2},{3,19},{19,3},{4,20},{20... | collective-permute-start | bytes 196616 | tf_op jit(solution)/shard_map/ppermute | solution.py:706
  6.2 11.1 %collective-permute-start.3 = (f32[14,8,128]{2,1,0:T(8,128)S(1)}, f32[14,8,128]{2,1,0:T(8,128)S(1)}, u32[]{:S(2)}, u32[]{:S(2)}) collective-permute-start(f32[14,8,128]{2,1,0:T(8,128)S(1)} %get-tuple-element.57), channel_id=1, source_target_pairs={{0,4},{1,2},{2,1},{3,7},{4,0},{5,6},{6,5},{7,3},{8,12},{9,10},{10,... | collective-permute-start | bytes 172040 | tf_op jit(solution)/shard_map/ppermute | solution.py:749
  6.3 5.5 %collective-permute-start.6 = (f32[4,8,128]{2,1,0:T(8,128)S(1)}, f32[4,8,128]{2,1,0:T(8,128)S(1)}, u32[]{:S(2)}, u32[]{:S(2)}) collective-permute-start(f32[4,8,128]{2,1,0:T(8,128)S(1)} %get-tuple-element.67.sent_small), channel_id=1, source_target_pairs={{0,1},{1,0},{2,3},{3,2},{4,5},{5,4},{6,7},{7,6},{8,9},{9,8},{10,11... | collective-permute-start | bytes 49160 | tf_op jit(solution)/shard_map/ppermute | solution.py:747
  9.9 7.4 %collective-permute-start.2 = (f32[12,8,128]{2,1,0:T(8,128)S(1)}, f32[12,8,128]{2,1,0:T(8,128)S(1)}, u32[]{:S(2)}, u32[]{:S(2)}) collective-permute-start(f32[12,8,128]{2,1,0:T(8,128)S(1)} %get-tuple-element.56), channel_id=1, source_target_pairs={{0,1},{1,0},{2,3},{3,2},{4,5},{5,4},{6,7},{7,6},{8,9},{9,8},{10,11... | collective-permute-start | bytes 147464 | tf_op jit(solution)/shard_map/ppermute | solution.py:748
  9.9 3.4 %collective-permute-start.5 = (f32[5,8,128]{2,1,0:T(8,128)S(1)}, f32[5,8,128]{2,1,0:T(8,128)S(1)}, u32[]{:S(2)}, u32[]{:S(2)}) collective-permute-start(f32[5,8,128]{2,1,0:T(8,128)S(1)} %get-tuple-element.66), channel_id=1, source_target_pairs={{0,12},{4,8},{8,4},{12,0},{1,13},{5,9},{9,5},{13,1},{2,14},{6,10},... | collective-permute-start | bytes 61448 | tf_op jit(solution)/shard_map/ppermute | solution.py:745
  11.8 1.5 %collective-permute-start.4 = (f32[5,8,128]{2,1,0:T(8,128)S(1)}, f32[5,8,128]{2,1,0:T(8,128)S(1)}, u32[]{:S(2)}, u32[]{:S(2)}) collective-permute-start(f32[5,8,128]{2,1,0:T(8,128)S(1)} %get-tuple-element.66), channel_id=1, source_target_pairs={{0,4},{4,0},{8,12},{12,8},{1,5},{5,1},{9,13},{13,9},{2,6},{6,2},{1... | collective-permute-start | bytes 61448 | tf_op jit(solution)/shard_map/ppermute | solution.py:744
  13.4 5.5 %collective-permute-start.7 = (f32[4,8,128]{2,1,0:T(8,128)S(1)}, f32[4,8,128]{2,1,0:T(8,128)S(1)}, u32[]{:S(2)}, u32[]{:S(2)}) collective-permute-start(f32[4,8,128]{2,1,0:T(8,128)S(1)} %relay.1), channel_id=1, source_target_pairs={{0,3},{1,2},{2,1},{3,0},{4,7},{5,6},{6,5},{7,4},{8,11},{9,10},{10,... | collective-permute-start | bytes 49160 | tf_op jit(solution)/shard_map/ppermute | solution.py:772
  15.9 1.4 %copy-start = (f32[4,8,8,128]{3,2,1,0:T(8,128)S(1)}, f32[4,8,8,128]{3,2,1,0:T(8,128)}, u32[]{:S(2)}) copy-start(f32[4,8,8,128]{3,2,1,0:T(8,128)} %material.1) | copy-start | bytes 393220

commit v2 on v1

--- a/solution.py
+++ b/solution.py
@@ -155,7 +155,7 @@
     solid, ocean, small, offset_x, offset_y, sems = refs[5:]
     copies = [
         pltpu.make_async_copy(solid_far, solid, sems.at[0]),
-        pltpu.make_async_copy(ocean_far, ocean, sems.at[1]),
+        pltpu.make_async_copy(ocean_far.at[pl.ds(0, 3)], ocean, sems.at[1]),
         pltpu.make_async_copy(medium_far, small, sems.at[2]),
         pltpu.make_async_copy(offset_x_far, offset_x, sems.at[3]),
         pltpu.make_async_copy(offset_y_far, offset_y, sems.at[4]),
@@ -677,7 +677,7 @@
         stage_kernel,
         out_shape=[
             pltpu.VMEM(solid_state.shape, f32),
-            pltpu.VMEM(ocean_state.shape, f32),
+            pltpu.VMEM((3, *ocean_state.shape[1:]), f32),
             pltpu.VMEM(ocean_medium.shape, f32),
             pltpu.VMEM((1, fine), jnp.int32),
             pltpu.VMEM((1, width), jnp.int32),
@@ -760,7 +760,7 @@
             dma((16,)),
         ],
         name="ocean",
-    )(ocean, medium, *got_x)
+    )(near(ocean_state), medium, *got_x)
 
     sent_far = pl.pallas_call(
         functools.partial(relay_kernel, count_x),

time: 20.2 us -> 20.2 us (level)
  no operation moved by 1% of the time
where the time goes in v2:
time: 20.2 us; the launch traced here: 20 us
  starting transfers between devices  9.33 us (46%)
  Pallas kernels  5.53 us (27%)
  waiting for transfers between devices  3.67 us (18%)
  between operations  0.74 us (4%)
  local copies, waits for them, and re-layouts  0.71 us (4%)
    ppermute x1, starting transfers between devices, compute(): got_small = near(lax.ppermute(sent_small, ring, even))  3.66 us
    ppermute x1, starting transfers between devices, compute(): planes = [lax.ppermute(plane, 'gx', p) for p in x_rounds]  2.97 us
    ppermute x1, starting transfers between devices, compute(): got_far = near(lax.ppermute(sent_far, ring, ends))  2.54 us
    ppermute x1, waiting for transfers between devices, compute(): got_small = near(lax.ppermute(sent_small, ring, even))  1.86 us
    ppermute x1, waiting for transfers between devices, compute(): got_yb = near(lax.ppermute(sent_y, 'gy', rounds_y[1]))  1.49 us
    pallas_call x1, Pallas kernels, compute(): pl.pallas_call(functools.partial(ocean_kernel, sizes), out_shape=[like(oc...  1.34 us
    pallas_call x1, Pallas kernels, compute(): pl.pallas_call(functools.partial(solid_kernel, sizes), out_shape=[like(so...  1.3 us
    pallas_call x1, Pallas kernels, compute(): pl.pallas_call(stage_kernel, out_shape=[pltpu.VMEM(solid_state.shape, f32...  1.13 us
  transfers between devices with their start and end apart: 8, of which 3 were waited for; matrix products, arithmetic and copies ran while one was open for 0% of the time, Pallas kernels for 22%

profile of v2, /device:TPU:0, one launch (start us, length us, event | category | flops | bytes accessed | tf_op | source)
XLA Modules:
  0.0 20.0 jit_solution(9033143935979366659)
XLA Ops:
  0.6 0.7 %slice_bitcast_fusion = f32[8,128]{1,0:T(8,128)S(1)} fusion(f32[9,8,8,128]{3,2,1,0:T(8,128)} %refs_0_.1), kind=kLoop, calls=%fused_computation | loop fusion | bytes 8192 | tf_op jit(solution)/shard_map/squeeze | solution.py:697
  1.3 3.0 %collective-permute-start = (f32[8,128]{1,0:T(8,128)S(1)}, f32[8,128]{1,0:T(8,128)S(1)}, u32[]{:S(2)}, u32[]{:S(2)}) collective-permute-start(f32[8,128]{1,0:T(8,128)S(1)} %slice_bitcast_fusion), channel_id=1, source_target_pairs={{0,16},{16,0},{1,17},{17,1},{2,18},{18,2},{3,19},{19,3},{4,20},{20... | collective-permute-start | bytes 12296 | tf_op jit(solution)/shard_map/ppermute | solution.py:698
  4.3 1.1 %stage.1 = (f32[9,8,8,128]{3,2,1,0:T(8,128)S(1)}, f32[3,16,16,64]{3,2,1,0:T(8,128)S(1)}, f32[2,16]{1,0:T(2,128)S(1)}, s32[1,16]{1,0:T(1,128)S(1)}, s32[1,64]{1,0:T(1,128)S(1)}) custom-call(f32[9,8,8,128]{3,2,1,0:T(8,128)} %refs_0_.1, f32[4,16,16,64]{3,2,1,0:T(8,128)} %ocean.3, f32[2,16]{1,0:T(2,128)} %refs_2_.1, s32[1,16]{1,0:T(1,128)} %bitcast.10, ...), custom_call_target="tpu_custom_call" | custom-call | tf_op jit(solution)/shard_map/stage/pallas_call | solution.py:676
  5.4 0.1 pack_x.1
  5.5 0.1 collective-permute-start.1
  5.6 0.3 %pack.1 = (f32[5,8,128]{2,1,0:T(8,128)S(1)}, f32[4,8,128]{2,1,0:T(8,128)S(1)}, f32[1,8,128]{2,1,0:T(8,128)S(1)}) custom-call(f32[9,8,8,128]{3,2,1,0:T(8,128)S(1)} %get-tuple-element.46.solid, f32[3,16,16,64]{3,2,1,0:T(8,128)S(1)} %get-tuple-element.47.ocean), custom_call_target="tpu_custom_call" | custom-call | tf_op jit(solution)/shard_map/pack/pallas_call | solution.py:707
  5.9 0.0 copy-start
  5.9 0.0 collective-permute-done.refs_0_
  5.9 0.2 %pack_z.1 = (f32[12,8,128]{2,1,0:T(8,128)S(1)}, f32[14,8,128]{2,1,0:T(8,128)S(1)}, f32[2,8,8,128]{3,2,1,0:T(8,128)S(1)}, s32[4,8,128]{2,1,0:T(8,128)S(1)}) custom-call(f32[9,8,8,128]{3,2,1,0:T(8,128)S(1)} %get-tuple-element.46.solid, f32[4,8,128]{2,1,0:T(8,128)S(1)} %get-tuple-element.67.sent_small, f32[2,16]{1,0:T(2,128)S(1)} %get-tuple-element.49.medium, ...), custom_call_target="tpu_custom_call" | custom-call | tf_op jit(solution)/shard_map/pack_z/pallas_call | solution.py:730
  6.1 0.1 collective-permute-start.3
  6.2 3.7 %collective-permute-start.6 = (f32[4,8,128]{2,1,0:T(8,128)S(1)}, f32[4,8,128]{2,1,0:T(8,128)S(1)}, u32[]{:S(2)}, u32[]{:S(2)}) collective-permute-start(f32[4,8,128]{2,1,0:T(8,128)S(1)} %get-tuple-element.67.sent_small), channel_id=1, source_target_pairs={{0,1},{1,0},{2,3},{3,2},{4,5},{5,4},{6,7},{7,6},{8,9},{9,8},{10,11... | collective-permute-start | bytes 49160 | tf_op jit(solution)/shard_map/ppermute | solution.py:747
  9.9 0.0 collective-permute-start.2
  9.9 0.0 collective-permute-start.5
  9.9 1.9 %collective-permute-done.6.got_small = f32[4,8,128]{2,1,0:T(8,128)S(1)} collective-permute-done((f32[4,8,128]{2,1,0:T(8,128)S(1)}, f32[4,8,128]{2,1,0:T(8,128)S(1)}, u32[]{:S(2)}, u32[]{:S(2)}) %collective-permute-start.6) | collective-permute-done | bytes 16416 | tf_op jit(solution)/shard_map/ppermute | solution.py:747
  11.8 0.0 collective-permute-start.4
  11.8 1.5 %collective-permute-done.5.got_yb = f32[5,8,128]{2,1,0:T(8,128)S(1)} collective-permute-done((f32[5,8,128]{2,1,0:T(8,128)S(1)}, f32[5,8,128]{2,1,0:T(8,128)S(1)}, u32[]{:S(2)}, u32[]{:S(2)}) %collective-permute-start.5) | collective-permute-done | bytes 20512 | tf_op jit(solution)/shard_map/ppermute | solution.py:745
  13.3 0.0 collective-permute-done.4.got_ya
  13.3 0.1 relay.1
  13.4 2.5 %collective-permute-start.7 = (f32[4,8,128]{2,1,0:T(8,128)S(1)}, f32[4,8,128]{2,1,0:T(8,128)S(1)}, u32[]{:S(2)}, u32[]{:S(2)}) collective-permute-start(f32[4,8,128]{2,1,0:T(8,128)S(1)} %relay.1), channel_id=1, source_target_pairs={{0,3},{1,2},{2,1},{3,0},{4,7},{5,6},{6,5},{7,4},{8,11},{9,10},{10,... | collective-permute-start | bytes 49160 | tf_op jit(solution)/shard_map/ppermute | solution.py:772
  15.9 0.0 collective-permute-done.1.refs_0_
  15.9 0.0 copy-done
  15.9 0.0 copy-start.1
  15.9 1.3 %ocean.2 = (f32[4,16,16,64]{3,2,1,0:T(8,128)}, f32[4,16,16,64]{3,2,1,0:T(8,128)}, f32[4,8,16,128]{3,2,1,0:T(8,128)S(1)}) custom-call(f32[4,16,16,64]{3,2,1,0:T(8,128)S(1)} %copy-done, f32[2,8,8,128]{3,2,1,0:T(8,128)S(1)} %get-tuple-element.52.medium, f32[16,8,128]{2,1,0:T(8,128)S(1)} %collective-permute-done.1.refs_0_), custom_call_target="tpu_custom_call" | custom-call | tf_op jit(solution)/shard_map/ocean/pallas_call | solution.py:751
  17.2 0.0 collective-permute-done.2.got_even
  17.3 0.0 collective-permute-done.3.got_odd
  17.3 0.0 copy-done.1
  17.3 1.3 %solid.1 = (f32[9,8,8,128]{3,2,1,0:T(8,128)}, f32[9,8,8,128]{3,2,1,0:T(8,128)}, f32[2,8,128]{2,1,0:T(8,128)S(1)}) custom-call(f32[9,8,8,128]{3,2,1,0:T(8,128)S(1)} %get-tuple-element.46.solid, f32[4,8,8,128]{3,2,1,0:T(8,128)S(1)} %copy-done.1, f32[12,8,128]{2,1,0:T(8,128)S(1)} %collective-permute-done.2.got_even, ...), custom_call_target="tpu_custom_call" | custom-call | tf_op jit(solution)/shard_map/solid/pallas_call | solution.py:774
  18.6 0.3 %collective-permute-done.7.got_far = f32[4,8,128]{2,1,0:T(8,128)S(1)} collective-permute-done((f32[4,8,128]{2,1,0:T(8,128)S(1)}, f32[4,8,128]{2,1,0:T(8,128)S(1)}, u32[]{:S(2)}, u32[]{:S(2)}) %collective-permute-start.7) | collective-permute-done | bytes 16416 | tf_op jit(solution)/shard_map/ppermute | solution.py:772
  18.9 1.1 %last.1 = (f32[9,8,8,128]{3,2,1,0:T(8,128)}, f32[9,8,8,128]{3,2,1,0:T(8,128)}, f32[4,16,16,64]{3,2,1,0:T(8,128)}, f32[4,16,16,64]{3,2,1,0:T(8,128)}) custom-call(f32[9,8,8,128]{3,2,1,0:T(8,128)S(1)} %get-tuple-element.46.solid, ...), custom_call_target="tpu_custom_call", output_to_operand_aliasing={{0}: (12, {}), {1}: (13, {}), {2}: (14, {}), {3}: (15, {})} | custom-call | tf_op jit(solution)/shard_map/last/pallas_call | solution.py:788
  (2 shorter events, 0.0 us)
Async XLA Ops:
  1.3 4.6 %collective-permute-start = (f32[8,128]{1,0:T(8,128)S(1)}, f32[8,128]{1,0:T(8,128)S(1)}, u32[]{:S(2)}, u32[]{:S(2)}) collective-permute-start(f32[8,128]{1,0:T(8,128)S(1)} %slice_bitcast_fusion), channel_id=1, source_target_pairs={{0,16},{16,0},{1,17},{17,1},{2,18},{18,2},{3,19},{19,3},{4,20},{20... | collective-permute-start | bytes 12296 | tf_op jit(solution)/shard_map/ppermute | solution.py:698
  5.5 10.4 %collective-permute-start.1 = (f32[16,8,128]{2,1,0:T(8,128)S(1)}, f32[16,8,128]{2,1,0:T(8,128)S(1)}, u32[]{:S(2)}, u32[]{:S(2)}) collective-permute-start(f32[16,8,128]{2,1,0:T(8,128)S(1)} %pack_x.1), channel_id=1, source_target_pairs={{0,16},{16,0},{1,17},{17,1},{2,18},{18,2},{3,19},{19,3},{4,20},{20... | collective-permute-start | bytes 196616 | tf_op jit(solution)/shard_map/ppermute | solution.py:706
  5.9 10.0 %copy-start = (f32[4,16,16,64]{3,2,1,0:T(8,128)S(1)}, f32[4,16,16,64]{3,2,1,0:T(8,128)}, u32[]{:S(2)}) copy-start(f32[4,16,16,64]{3,2,1,0:T(8,128)} %ocean.3) | copy-start | bytes 786436
  6.1 11.1 %collective-permute-start.3 = (f32[14,8,128]{2,1,0:T(8,128)S(1)}, f32[14,8,128]{2,1,0:T(8,128)S(1)}, u32[]{:S(2)}, u32[]{:S(2)}) collective-permute-start(f32[14,8,128]{2,1,0:T(8,128)S(1)} %get-tuple-element.57), channel_id=1, source_target_pairs={{0,4},{1,2},{2,1},{3,7},{4,0},{5,6},{6,5},{7,3},{8,12},{9,10},{10,... | collective-permute-start | bytes 172040 | tf_op jit(solution)/shard_map/ppermute | solution.py:749
  6.2 5.5 %collective-permute-start.6 = (f32[4,8,128]{2,1,0:T(8,128)S(1)}, f32[4,8,128]{2,1,0:T(8,128)S(1)}, u32[]{:S(2)}, u32[]{:S(2)}) collective-permute-start(f32[4,8,128]{2,1,0:T(8,128)S(1)} %get-tuple-element.67.sent_small), channel_id=1, source_target_pairs={{0,1},{1,0},{2,3},{3,2},{4,5},{5,4},{6,7},{7,6},{8,9},{9,8},{10,11... | collective-permute-start | bytes 49160 | tf_op jit(solution)/shard_map/ppermute | solution.py:747
  9.9 7.4 %collective-permute-start.2 = (f32[12,8,128]{2,1,0:T(8,128)S(1)}, f32[12,8,128]{2,1,0:T(8,128)S(1)}, u32[]{:S(2)}, u32[]{:S(2)}) collective-permute-start(f32[12,8,128]{2,1,0:T(8,128)S(1)} %get-tuple-element.56), channel_id=1, source_target_pairs={{0,1},{1,0},{2,3},{3,2},{4,5},{5,4},{6,7},{7,6},{8,9},{9,8},{10,11... | collective-permute-start | bytes 147464 | tf_op jit(solution)/shard_map/ppermute | solution.py:748
  9.9 3.4 %collective-permute-start.5 = (f32[5,8,128]{2,1,0:T(8,128)S(1)}, f32[5,8,128]{2,1,0:T(8,128)S(1)}, u32[]{:S(2)}, u32[]{:S(2)}) collective-permute-start(f32[5,8,128]{2,1,0:T(8,128)S(1)} %get-tuple-element.66), channel_id=1, source_target_pairs={{0,12},{4,8},{8,4},{12,0},{1,13},{5,9},{9,5},{13,1},{2,14},{6,10},... | collective-permute-start | bytes 61448 | tf_op jit(solution)/shard_map/ppermute | solution.py:745
  11.8 1.5 %collective-permute-start.4 = (f32[5,8,128]{2,1,0:T(8,128)S(1)}, f32[5,8,128]{2,1,0:T(8,128)S(1)}, u32[]{:S(2)}, u32[]{:S(2)}) collective-permute-start(f32[5,8,128]{2,1,0:T(8,128)S(1)} %get-tuple-element.66), channel_id=1, source_target_pairs={{0,4},{4,0},{8,12},{12,8},{1,5},{5,1},{9,13},{13,9},{2,6},{6,2},{1... | collective-permute-start | bytes 61448 | tf_op jit(solution)/shard_map/ppermute | solution.py:744
  13.4 5.5 %collective-permute-start.7 = (f32[4,8,128]{2,1,0:T(8,128)S(1)}, f32[4,8,128]{2,1,0:T(8,128)S(1)}, u32[]{:S(2)}, u32[]{:S(2)}) collective-permute-start(f32[4,8,128]{2,1,0:T(8,128)S(1)} %relay.1), channel_id=1, source_target_pairs={{0,3},{1,2},{2,1},{3,0},{4,7},{5,6},{6,5},{7,4},{8,11},{9,10},{10,... | collective-permute-start | bytes 49160 | tf_op jit(solution)/shard_map/ppermute | solution.py:772
  15.9 1.4 %copy-start.1 = (f32[4,8,8,128]{3,2,1,0:T(8,128)S(1)}, f32[4,8,8,128]{3,2,1,0:T(8,128)}, u32[]{:S(2)}) copy-start(f32[4,8,8,128]{3,2,1,0:T(8,128)} %material.1) | copy-start | bytes 393220

commit v3 on v1

--- a/solution.py
+++ b/solution.py
@@ -394,8 +394,6 @@
             rate_w = rate_w - jnp.where(lower, inv_norm * light * p, 0.0)
         carry[0, k] = rate_p
         carry[1, k] = -2.0 * light * dyp
-        carry[2, k] = p
-        carry[3, k] = v
         store_pair(stage_rate, stage_next, 0, k, -2.0 * light * dxp, u)
         store_pair(stage_rate, stage_next, 1, k, rate_w, w)
         if (k + 1) % chunk == 0:
@@ -565,7 +563,7 @@
 
 
 def last_kernel(
-    sizes, solid, medium, pressure, index, ocean_carry, solid_carry,
+    sizes, solid, ocean, medium, pressure, index, ocean_carry, solid_carry,
     got_small, got_odd, got_far, got_ya, got_yb, *refs,
 ):
     _, span_y, span_z = sizes
@@ -636,7 +634,12 @@
             rate = ocean_carry[slot, k] - 2.0 * scale * ends
             if slot == 0 and k == pairs - 1:
                 rate = rate - pull
-            store_pair(stage_rate, stage_next, slot, k, rate, ocean_carry[2 + slot, k])
+            rate = step_size * rate
+            for level, part in ((k, rate), (k + pairs, turn(rate, half, 1))):
+                stage_rate[slot, level] = part[:, :half]
+                stage_next[slot, level] = (
+                    ocean[field, level] + section_weight * part[:, :half]
+                )
         fresh = [
             pltpu.make_async_copy(stage.at[slot], out.at[field], sems.at[len(copies) + i])
             for i, (stage, out) in enumerate(
@@ -750,7 +753,7 @@
 
     ocean_next, ocean_rate, ocean_carry = pl.pallas_call(
         functools.partial(ocean_kernel, sizes),
-        out_shape=[like(ocean_state), like(ocean_state), pltpu.VMEM((4, pairs, fine, lanes), f32)],
+        out_shape=[like(ocean_state), like(ocean_state), pltpu.VMEM((2, pairs, fine, lanes), f32)],
         in_specs=[vmem] * (2 + count_x),
         out_specs=[hbm, hbm, vmem],
         scratch_shapes=[
@@ -788,9 +791,9 @@
     return pl.pallas_call(
         functools.partial(last_kernel, sizes),
         out_shape=[like(solid_state), like(solid_state), like(ocean_state), like(ocean_state)],
-        in_specs=[vmem] * (11 + count_x) + [hbm] * 4,
+        in_specs=[vmem] * (12 + count_x) + [hbm] * 4,
         out_specs=[hbm] * 4,
-        input_output_aliases={11 + count_x + i: i for i in range(4)},
+        input_output_aliases={12 + count_x + i: i for i in range(4)},
         scratch_shapes=[
             pltpu.VMEM((2, levels, fine, width), f32),
             pltpu.VMEM((2, levels, fine, width), f32),
@@ -800,7 +803,7 @@
         ],
         name="last",
     )(
-        solid, medium, pressure, index, near(ocean_carry), near(solid_carry),
+        solid, ocean, medium, pressure, index, near(ocean_carry), near(solid_carry),
         got_small, got_odd, got_far, *got_y, *planes,
         solid_next, solid_rate, ocean_next, ocean_rate,
     )

time: 20.2 us -> 20.2 us (level)
  no operation moved by 1% of the time
where the time goes in v3:
time: 20.2 us; the launch traced here: 20 us
  starting transfers between devices  9.33 us (46%)
  Pallas kernels  5.59 us (28%)
  waiting for transfers between devices  3.67 us (18%)
  between operations  0.73 us (4%)
  local copies, waits for them, and re-layouts  0.7 us (3%)
    ppermute x1, starting transfers between devices, compute(): got_small = near(lax.ppermute(sent_small, ring, even))  3.66 us
    ppermute x1, starting transfers between devices, compute(): planes = [lax.ppermute(plane, 'gx', p) for p in x_rounds]  2.97 us
    ppermute x1, starting transfers between devices, compute(): got_far = near(lax.ppermute(sent_far, ring, ends))  2.54 us
    ppermute x1, waiting for transfers between devices, compute(): got_small = near(lax.ppermute(sent_small, ring, even))  1.86 us
    ppermute x1, waiting for transfers between devices, compute(): got_yb = near(lax.ppermute(sent_y, 'gy', rounds_y[1]))  1.49 us
    pallas_call x1, Pallas kernels, compute(): pl.pallas_call(functools.partial(ocean_kernel, sizes), out_shape=[like(oc...  1.34 us
    pallas_call x1, Pallas kernels, compute(): pl.pallas_call(functools.partial(solid_kernel, sizes), out_shape=[like(so...  1.3 us
    pallas_call x1, Pallas kernels, compute(): pl.pallas_call(stage_kernel, out_shape=[pltpu.VMEM(solid_state.shape, f32...  1.18 us
  transfers between devices with their start and end apart: 8, of which 3 were waited for; matrix products, arithmetic and copies ran while one was open for 0% of the time, Pallas kernels for 22%

profile of v3, /device:TPU:0, one launch (start us, length us, event | category | flops | bytes accessed | tf_op | source)
XLA Modules:
  0.0 20.0 jit_solution(38892799440736976)
XLA Ops:
  0.6 0.7 %slice_bitcast_fusion = f32[8,128]{1,0:T(8,128)S(1)} fusion(f32[9,8,8,128]{3,2,1,0:T(8,128)} %refs_0_.1), kind=kLoop, calls=%fused_computation | loop fusion | bytes 8192 | tf_op jit(solution)/shard_map/squeeze | solution.py:700
  1.3 3.0 %collective-permute-start = (f32[8,128]{1,0:T(8,128)S(1)}, f32[8,128]{1,0:T(8,128)S(1)}, u32[]{:S(2)}, u32[]{:S(2)}) collective-permute-start(f32[8,128]{1,0:T(8,128)S(1)} %slice_bitcast_fusion), channel_id=1, source_target_pairs={{0,16},{16,0},{1,17},{17,1},{2,18},{18,2},{3,19},{19,3},{4,20},{20... | collective-permute-start | bytes 12296 | tf_op jit(solution)/shard_map/ppermute | solution.py:701
  4.3 1.2 %stage.1 = (f32[9,8,8,128]{3,2,1,0:T(8,128)S(1)}, f32[4,16,16,64]{3,2,1,0:T(8,128)S(1)}, f32[2,16]{1,0:T(2,128)S(1)}, s32[1,16]{1,0:T(1,128)S(1)}, s32[1,64]{1,0:T(1,128)S(1)}) custom-call(f32[9,8,8,128]{3,2,1,0:T(8,128)} %refs_0_.1, f32[4,16,16,64]{3,2,1,0:T(8,128)} %refs_1_.1, f32[2,16]{1,0:T(2,128)} %refs_2_.1, s32[1,16]{1,0:T(1,128)} %bitcast.10, ...), custom_call_target="tpu_custom_call" | custom-call | tf_op jit(solution)/shard_map/stage/pallas_call | solution.py:679
  5.5 0.1 pack_x.1
  5.6 0.1 collective-permute-start.1
  5.7 0.3 %pack.1 = (f32[5,8,128]{2,1,0:T(8,128)S(1)}, f32[4,8,128]{2,1,0:T(8,128)S(1)}, f32[1,8,128]{2,1,0:T(8,128)S(1)}) custom-call(f32[9,8,8,128]{3,2,1,0:T(8,128)S(1)} %get-tuple-element.46.solid, f32[4,16,16,64]{3,2,1,0:T(8,128)S(1)} %get-tuple-element.47.ocean), custom_call_target="tpu_custom_call" | custom-call | tf_op jit(solution)/shard_map/pack/pallas_call | solution.py:710
  5.9 0.0 collective-permute-done.refs_0_
  6.0 0.2 %pack_z.1 = (f32[12,8,128]{2,1,0:T(8,128)S(1)}, f32[14,8,128]{2,1,0:T(8,128)S(1)}, f32[2,8,8,128]{3,2,1,0:T(8,128)S(1)}, s32[4,8,128]{2,1,0:T(8,128)S(1)}) custom-call(f32[9,8,8,128]{3,2,1,0:T(8,128)S(1)} %get-tuple-element.46.solid, f32[4,8,128]{2,1,0:T(8,128)S(1)} %get-tuple-element.67.sent_small, f32[2,16]{1,0:T(2,128)S(1)} %get-tuple-element.49.medium, ...), custom_call_target="tpu_custom_call" | custom-call | tf_op jit(solution)/shard_map/pack_z/pallas_call | solution.py:733
  6.2 0.1 collective-permute-start.3
  6.3 3.7 %collective-permute-start.6 = (f32[4,8,128]{2,1,0:T(8,128)S(1)}, f32[4,8,128]{2,1,0:T(8,128)S(1)}, u32[]{:S(2)}, u32[]{:S(2)}) collective-permute-start(f32[4,8,128]{2,1,0:T(8,128)S(1)} %get-tuple-element.67.sent_small), channel_id=1, source_target_pairs={{0,1},{1,0},{2,3},{3,2},{4,5},{5,4},{6,7},{7,6},{8,9},{9,8},{10,11... | collective-permute-start | bytes 49160 | tf_op jit(solution)/shard_map/ppermute | solution.py:750
  9.9 0.0 collective-permute-start.2
  9.9 0.0 collective-permute-start.5
  10.0 1.9 %collective-permute-done.6.got_small = f32[4,8,128]{2,1,0:T(8,128)S(1)} collective-permute-done((f32[4,8,128]{2,1,0:T(8,128)S(1)}, f32[4,8,128]{2,1,0:T(8,128)S(1)}, u32[]{:S(2)}, u32[]{:S(2)}) %collective-permute-start.6) | collective-permute-done | bytes 16416 | tf_op jit(solution)/shard_map/ppermute | solution.py:750
  11.8 0.0 collective-permute-start.4
  11.8 1.5 %collective-permute-done.5.got_yb = f32[5,8,128]{2,1,0:T(8,128)S(1)} collective-permute-done((f32[5,8,128]{2,1,0:T(8,128)S(1)}, f32[5,8,128]{2,1,0:T(8,128)S(1)}, u32[]{:S(2)}, u32[]{:S(2)}) %collective-permute-start.5) | collective-permute-done | bytes 20512 | tf_op jit(solution)/shard_map/ppermute | solution.py:748
  13.3 0.0 collective-permute-done.4.got_ya
  13.3 0.1 relay.1
  13.4 2.5 %collective-permute-start.7 = (f32[4,8,128]{2,1,0:T(8,128)S(1)}, f32[4,8,128]{2,1,0:T(8,128)S(1)}, u32[]{:S(2)}, u32[]{:S(2)}) collective-permute-start(f32[4,8,128]{2,1,0:T(8,128)S(1)} %relay.1), channel_id=1, source_target_pairs={{0,3},{1,2},{2,1},{3,0},{4,7},{5,6},{6,5},{7,4},{8,11},{9,10},{10,... | collective-permute-start | bytes 49160 | tf_op jit(solution)/shard_map/ppermute | solution.py:775
  15.9 0.0 collective-permute-done.1.refs_0_
  15.9 0.0 copy-start
  15.9 1.3 %ocean.1 = (f32[4,16,16,64]{3,2,1,0:T(8,128)}, f32[4,16,16,64]{3,2,1,0:T(8,128)}, f32[2,8,16,128]{3,2,1,0:T(8,128)S(1)}) custom-call(f32[4,16,16,64]{3,2,1,0:T(8,128)S(1)} %get-tuple-element.47.ocean, f32[2,8,8,128]{3,2,1,0:T(8,128)S(1)} %get-tuple-element.52.medium, f32[16,8,128]{2,1,0:T(8,128)S(1)} %collective-permute-done.1.refs_0_), custom_call_target="tpu_custom_call" | custom-call | tf_op jit(solution)/shard_map/ocean/pallas_call | solution.py:754
  17.3 0.0 collective-permute-done.2.got_even
  17.3 0.0 collective-permute-done.3.got_odd
  17.3 0.0 copy-done
  17.3 1.3 %solid.1 = (f32[9,8,8,128]{3,2,1,0:T(8,128)}, f32[9,8,8,128]{3,2,1,0:T(8,128)}, f32[2,8,128]{2,1,0:T(8,128)S(1)}) custom-call(f32[9,8,8,128]{3,2,1,0:T(8,128)S(1)} %get-tuple-element.46.solid, f32[4,8,8,128]{3,2,1,0:T(8,128)S(1)} %copy-done, f32[12,8,128]{2,1,0:T(8,128)S(1)} %collective-permute-done.2.got_even, ...), custom_call_target="tpu_custom_call" | custom-call | tf_op jit(solution)/shard_map/solid/pallas_call | solution.py:777
  18.6 0.3 %collective-permute-done.7.got_far = f32[4,8,128]{2,1,0:T(8,128)S(1)} collective-permute-done((f32[4,8,128]{2,1,0:T(8,128)S(1)}, f32[4,8,128]{2,1,0:T(8,128)S(1)}, u32[]{:S(2)}, u32[]{:S(2)}) %collective-permute-start.7) | collective-permute-done | bytes 16416 | tf_op jit(solution)/shard_map/ppermute | solution.py:775
  18.9 1.1 %last.1 = (f32[9,8,8,128]{3,2,1,0:T(8,128)}, f32[9,8,8,128]{3,2,1,0:T(8,128)}, f32[4,16,16,64]{3,2,1,0:T(8,128)}, f32[4,16,16,64]{3,2,1,0:T(8,128)}) custom-call(f32[9,8,8,128]{3,2,1,0:T(8,128)S(1)} %get-tuple-element.46.solid, ...), custom_call_target="tpu_custom_call", output_to_operand_aliasing={{0}: (13, {}), {1}: (14, {}), {2}: (15, {}), {3}: (16, {})} | custom-call | tf_op jit(solution)/shard_map/last/pallas_call | solution.py:791
  (2 shorter events, 0.0 us)
Async XLA Ops:
  1.3 4.6 %collective-permute-start = (f32[8,128]{1,0:T(8,128)S(1)}, f32[8,128]{1,0:T(8,128)S(1)}, u32[]{:S(2)}, u32[]{:S(2)}) collective-permute-start(f32[8,128]{1,0:T(8,128)S(1)} %slice_bitcast_fusion), channel_id=1, source_target_pairs={{0,16},{16,0},{1,17},{17,1},{2,18},{18,2},{3,19},{19,3},{4,20},{20... | collective-permute-start | bytes 12296 | tf_op jit(solution)/shard_map/ppermute | solution.py:701
  5.6 10.3 %collective-permute-start.1 = (f32[16,8,128]{2,1,0:T(8,128)S(1)}, f32[16,8,128]{2,1,0:T(8,128)S(1)}, u32[]{:S(2)}, u32[]{:S(2)}) collective-permute-start(f32[16,8,128]{2,1,0:T(8,128)S(1)} %pack_x.1), channel_id=1, source_target_pairs={{0,16},{16,0},{1,17},{17,1},{2,18},{18,2},{3,19},{19,3},{4,20},{20... | collective-permute-start | bytes 196616 | tf_op jit(solution)/shard_map/ppermute | solution.py:709
  6.2 11.1 %collective-permute-start.3 = (f32[14,8,128]{2,1,0:T(8,128)S(1)}, f32[14,8,128]{2,1,0:T(8,128)S(1)}, u32[]{:S(2)}, u32[]{:S(2)}) collective-permute-start(f32[14,8,128]{2,1,0:T(8,128)S(1)} %get-tuple-element.57), channel_id=1, source_target_pairs={{0,4},{1,2},{2,1},{3,7},{4,0},{5,6},{6,5},{7,3},{8,12},{9,10},{10,... | collective-permute-start | bytes 172040 | tf_op jit(solution)/shard_map/ppermute | solution.py:752
  6.3 5.5 %collective-permute-start.6 = (f32[4,8,128]{2,1,0:T(8,128)S(1)}, f32[4,8,128]{2,1,0:T(8,128)S(1)}, u32[]{:S(2)}, u32[]{:S(2)}) collective-permute-start(f32[4,8,128]{2,1,0:T(8,128)S(1)} %get-tuple-element.67.sent_small), channel_id=1, source_target_pairs={{0,1},{1,0},{2,3},{3,2},{4,5},{5,4},{6,7},{7,6},{8,9},{9,8},{10,11... | collective-permute-start | bytes 49160 | tf_op jit(solution)/shard_map/ppermute | solution.py:750
  9.9 7.4 %collective-permute-start.2 = (f32[12,8,128]{2,1,0:T(8,128)S(1)}, f32[12,8,128]{2,1,0:T(8,128)S(1)}, u32[]{:S(2)}, u32[]{:S(2)}) collective-permute-start(f32[12,8,128]{2,1,0:T(8,128)S(1)} %get-tuple-element.56), channel_id=1, source_target_pairs={{0,1},{1,0},{2,3},{3,2},{4,5},{5,4},{6,7},{7,6},{8,9},{9,8},{10,11... | collective-permute-start | bytes 147464 | tf_op jit(solution)/shard_map/ppermute | solution.py:751
  9.9 3.4 %collective-permute-start.5 = (f32[5,8,128]{2,1,0:T(8,128)S(1)}, f32[5,8,128]{2,1,0:T(8,128)S(1)}, u32[]{:S(2)}, u32[]{:S(2)}) collective-permute-start(f32[5,8,128]{2,1,0:T(8,128)S(1)} %get-tuple-element.66), channel_id=1, source_target_pairs={{0,12},{4,8},{8,4},{12,0},{1,13},{5,9},{9,5},{13,1},{2,14},{6,10},... | collective-permute-start | bytes 61448 | tf_op jit(solution)/shard_map/ppermute | solution.py:748
  11.8 1.5 %collective-permute-start.4 = (f32[5,8,128]{2,1,0:T(8,128)S(1)}, f32[5,8,128]{2,1,0:T(8,128)S(1)}, u32[]{:S(2)}, u32[]{:S(2)}) collective-permute-start(f32[5,8,128]{2,1,0:T(8,128)S(1)} %get-tuple-element.66), channel_id=1, source_target_pairs={{0,4},{4,0},{8,12},{12,8},{1,5},{5,1},{9,13},{13,9},{2,6},{6,2},{1... | collective-permute-start | bytes 61448 | tf_op jit(solution)/shard_map/ppermute | solution.py:747
  13.4 5.5 %collective-permute-start.7 = (f32[4,8,128]{2,1,0:T(8,128)S(1)}, f32[4,8,128]{2,1,0:T(8,128)S(1)}, u32[]{:S(2)}, u32[]{:S(2)}) collective-permute-start(f32[4,8,128]{2,1,0:T(8,128)S(1)} %relay.1), channel_id=1, source_target_pairs={{0,3},{1,2},{2,1},{3,0},{4,7},{5,6},{6,5},{7,4},{8,11},{9,10},{10,... | collective-permute-start | bytes 49160 | tf_op jit(solution)/shard_map/ppermute | solution.py:775
  15.9 1.4 %copy-start = (f32[4,8,8,128]{3,2,1,0:T(8,128)S(1)}, f32[4,8,8,128]{3,2,1,0:T(8,128)}, u32[]{:S(2)}) copy-start(f32[4,8,8,128]{3,2,1,0:T(8,128)} %material.1) | copy-start | bytes 393220
